TPU v7x, 256 devices: a whole 4x4x8 slice. The times are simulated.
256 devices in a mesh: ctx: 64 (over x_lo, z, y), head: 4 (over x_hi, core).
Axes of the slice: x: 4 (x_hi: 2, x_lo: 2; x = x_hi * 2 + x_lo), y: 4, z: 8, core: 2. Of those that a mesh axis runs over, the one named last changes fastest.
Arguments:
- query_local: bfloat16 [12288, 5120], P(('ctx', 'head')), may hold values from -6 to 6
- key_local: bfloat16 [12288, 1024], P(('ctx', 'head')), may hold values from -6 to 6
- value_local: bfloat16 [12288, 1024], P(('ctx', 'head')), may hold values from -6 to 6
- stretch_labels: int32 [12288], replicated, may hold values from 0 to 31, never falling along the last dimension, each value on 1 to 768 neighbouring positions
- query_global: bfloat16 [12288, 5120], P(('ctx', 'head')), may hold values from -5 to 5
- key_global: bfloat16 [12288, 1024], P(('ctx', 'head')), may hold values from -5 to 5
- value_global: bfloat16 [12288, 1024], P(('ctx', 'head')), may hold values from -6 to 6
Outputs:
- local_heads: bfloat16 [12288, 5120], P(('ctx', 'head'))
- global_heads: bfloat16 [12288, 5120], P(('ctx', 'head'))
Inputs may be any that keep to these rules, and one draw needn't show every extreme that they name: `stretch_labels`: stretches are runs of consecutive tokens; numbers never fall; each stretch has 1 to 768 tokens and some stretch has exactly 768.
All inputs are finite; a program needn't handle non-finite values.
Results may differ from a plain program's by a relative error of at most 0.0059.
Values may be sent and summed in bfloat16 or wider, within the bound.
A program may use at most 128 MiB of HBM per device.

v0:
```python
import jax
import jax.numpy as jnp
from jax import lax
from jax.sharding import PartitionSpec as P

HEAD = 128
STRETCH_SPAN = 4


rope_base = 500000.0
norm_epsilon = 1e-06
temper_floor = 8192
temper_slope = 0.1
masked_score = -1e30


def passed_along(shard, axis, by):
    size = lax.axis_size(axis)
    pairs = [(i, i + by) for i in range(size) if 0 <= i + by < size]
    return lax.ppermute(shard, axis, pairs)


def swapped(shard, axis, distance):
    return lax.ppermute(shard, axis, [(i, i ^ 1 << distance) for i in range(lax.axis_size(axis))])


def in_one_piece(arrays, axis, dim, along):
    both = jnp.concatenate(arrays, axis=along)
    result, at, gathered = (lax.all_gather(both, axis, axis=dim, tiled=True), 0, [])
    for a in arrays:
        gathered.append(lax.slice_in_dim(result, at, at + a.shape[along], axis=along))
        at += a.shape[along]
    return tuple(gathered)


def rotate(tensor, positions):
    head_width = tensor.shape[-1]
    half_width = head_width // 2
    frequency = rope_base ** (-(jnp.arange(half_width, dtype=jnp.float32) * 2.0 / head_width))
    angles = positions.astype(jnp.float32)[:, None] * frequency[None, :]
    extra_dims = tensor.ndim - 2
    angles = angles.reshape((angles.shape[0],) + (1,) * extra_dims + (half_width,))
    cosine = jnp.cos(angles)
    sine_part = jnp.sin(angles)
    first_part = tensor[..., :half_width]
    second_part = tensor[..., half_width:]
    return jnp.concatenate(
        [
            first_part * cosine - second_part * sine_part,
            first_part * sine_part + second_part * cosine,
        ],
        axis=-1,
    )


def normalize(tensor):
    return tensor * lax.rsqrt(jnp.mean(tensor * tensor, axis=-1, keepdims=True) + norm_epsilon)


def tempering(positions):
    return 1.0 + temper_slope * jnp.log(((positions + 1) // temper_floor + 1).astype(jnp.float32))


def local_update(
    running, queries, query_ids, query_pos, key_block, value_block, key_ids, key_pos, scaling
):
    allowed = (key_ids[None, :] == query_ids[:, None]) & (key_pos[None, :] <= query_pos[:, None])

    def update(carried):
        weighted, totals = carried
        scores = (
            jnp.einsum("qhgd,khd->hgqk", queries, key_block, preferred_element_type=jnp.float32)
            * scaling
        )
        weights = jnp.where(allowed[None, None], jnp.exp(scores), 0.0)
        totals = totals + jnp.sum(weights, axis=-1)
        weighted = weighted + jnp.einsum(
            "hgqk,khd->qhgd",
            weights.astype(jnp.bfloat16),
            value_block,
            preferred_element_type=jnp.float32,
        )
        return (weighted, totals)

    return lax.cond(jnp.any(allowed), update, lambda carried: carried, running)


def global_update(running, queries, query_pos, query_scale, key_block, value_block, key_pos):
    allowed = key_pos[None, :] <= query_pos[:, None]

    def update(carried):
        row_peak, totals, weighted = carried
        scores = (
            jnp.einsum("qhgd,khd->hgqk", queries, key_block, preferred_element_type=jnp.float32)
            * query_scale[None, None, :, None]
        )
        scores = jnp.where(allowed[None, None], scores, masked_score)
        new_peak = jnp.maximum(row_peak, jnp.max(scores, axis=-1))
        weights = jnp.where(allowed[None, None], jnp.exp(scores - new_peak[..., None]), 0.0)
        factor = jnp.exp(row_peak - new_peak)
        totals = totals * factor + jnp.sum(weights, axis=-1)
        weighted = weighted * jnp.transpose(factor, (2, 0, 1))[..., None] + jnp.einsum(
            "hgqk,khd->qhgd",
            weights.astype(jnp.bfloat16),
            value_block,
            preferred_element_type=jnp.float32,
        )
        return (new_peak, totals, weighted)

    return lax.cond(jnp.any(allowed), update, lambda carried: carried, running)


def shards(
    query_local, key_local, value_local, stretch_labels, query_global, key_global, value_global
):
    ctx_count = lax.axis_size("ctx")
    ctx_index = lax.axis_index("ctx")
    query_local, key_local, value_local, query_global, key_global, value_global = (
        lax.all_to_all(query_local, "head", split_axis=1, concat_axis=0, tiled=True),
        lax.all_to_all(key_local, "head", split_axis=1, concat_axis=0, tiled=True),
        lax.all_to_all(value_local, "head", split_axis=1, concat_axis=0, tiled=True),
        lax.all_to_all(query_global, "head", split_axis=1, concat_axis=0, tiled=True),
        lax.all_to_all(key_global, "head", split_axis=1, concat_axis=0, tiled=True),
        lax.all_to_all(value_global, "head", split_axis=1, concat_axis=0, tiled=True),
    )
    tokens = query_local.shape[0]
    half_rows = tokens // 2
    key_heads = key_local.shape[1] // HEAD
    group_size = query_local.shape[1] // (key_heads * HEAD)
    scaling = HEAD ** (-0.5)
    query_shape = (tokens, key_heads, group_size, HEAD)
    key_shape = (tokens, key_heads, HEAD)
    offsets = jnp.arange(tokens, dtype=jnp.int32)
    positions = ctx_index * tokens + offsets
    queries = normalize(
        rotate(query_local.astype(jnp.float32).reshape(query_shape), positions)
    ).astype(jnp.bfloat16)
    keys_normed = normalize(
        rotate(key_local.astype(jnp.float32).reshape(key_shape), positions)
    ).astype(jnp.bfloat16)
    values_local = value_local.reshape(key_shape)
    query_ids = lax.dynamic_slice_in_dim(stretch_labels, ctx_index * tokens, tokens, 0)
    local_state = (
        jnp.zeros(query_shape, jnp.float32),
        jnp.zeros((key_heads, group_size, tokens), jnp.float32),
    )
    local_state = local_update(
        local_state,
        queries,
        query_ids,
        positions,
        keys_normed,
        values_local,
        query_ids,
        positions,
        scaling,
    )
    source = (keys_normed, values_local)
    for distance in range(1, STRETCH_SPAN + 1):
        source = passed_along((source[0], source[1]), "ctx", 1)
        first_row = (ctx_index - distance) * tokens
        key_ids = lax.dynamic_slice_in_dim(stretch_labels, jnp.maximum(first_row, 0), tokens, 0)
        key_ids = jnp.where(first_row >= 0, key_ids, -1)
        local_state = local_update(
            local_state,
            queries,
            query_ids,
            positions,
            source[0],
            source[1],
            key_ids,
            first_row + offsets,
            scaling,
        )
    weighted, totals = local_state
    local_heads = (
        (weighted / jnp.transpose(totals, (2, 0, 1))[..., None])
        .astype(jnp.bfloat16)
        .reshape(tokens, -1)
    )
    bit_count = ctx_count.bit_length() - 1
    moving = swapped(query_global[half_rows:], "ctx", bit_count - 1)
    query_halves = (query_global[:half_rows], moving)
    partner = jnp.bitwise_xor(ctx_index, ctx_count // 2)
    query_pos = jnp.concatenate(
        [positions[:half_rows], partner * tokens + offsets[half_rows:]], axis=0
    )
    query_parts = []
    for branch in range(2):
        part_pos = query_pos[branch * half_rows : (branch + 1) * half_rows]
        query_parts.append(
            (
                query_halves[branch].reshape(half_rows, key_heads, group_size, HEAD),
                part_pos,
                tempering(part_pos) * scaling,
            )
        )
    initial = (
        jnp.full((key_heads, group_size, half_rows), masked_score, jnp.float32),
        jnp.zeros((key_heads, group_size, half_rows), jnp.float32),
        jnp.zeros((half_rows, key_heads, group_size, HEAD), jnp.float32),
    )

    def absorb(carried, key_block, value_block, block_pos):
        return tuple(
            (
                global_update(
                    carried[member],
                    query_parts[member][0],
                    query_parts[member][1],
                    query_parts[member][2],
                    key_block,
                    value_block,
                    block_pos,
                )
                for member in range(2)
            )
        )

    key_piece, value_piece = in_one_piece((key_global, value_global), "ctx", 0, 1)
    piece_rows = key_piece.shape[0]
    key_piece = key_piece.reshape(piece_rows, key_heads, HEAD)
    value_piece = value_piece.reshape(piece_rows, key_heads, HEAD)
    key_pos = jnp.arange(piece_rows, dtype=jnp.int32)

    def advance(number, running):
        anchor = number * half_rows
        return absorb(
            running,
            lax.dynamic_slice_in_dim(key_piece, anchor, half_rows, 0),
            lax.dynamic_slice_in_dim(value_piece, anchor, half_rows, 0),
            lax.dynamic_slice_in_dim(key_pos, anchor, half_rows, 0),
        )

    states = lax.fori_loop(0, piece_rows // half_rows, advance, (initial, initial))
    output_halves = []
    for branch in range(2):
        row_peak, totals, weighted = states[branch]
        output_halves.append(
            (weighted / jnp.transpose(totals, (2, 0, 1))[..., None])
            .astype(jnp.bfloat16)
            .reshape(half_rows, -1)
        )
    output_halves[1] = swapped(output_halves[1], "ctx", bit_count - 1)
    global_heads = jnp.concatenate(output_halves, axis=0)
    return (
        lax.all_to_all(local_heads, "head", split_axis=0, concat_axis=1, tiled=True),
        lax.all_to_all(global_heads, "head", split_axis=0, concat_axis=1, tiled=True),
    )


def solution(mesh):
    return jax.shard_map(
        shards,
        mesh=mesh,
        in_specs=(
            P(("ctx", "head"), None),
            P(("ctx", "head"), None),
            P(("ctx", "head"), None),
            P(),
            P(("ctx", "head"), None),
            P(("ctx", "head"), None),
            P(("ctx", "head"), None),
        ),
        out_specs=(P(("ctx", "head"), None), P(("ctx", "head"), None)),
        check_vma=False,
    )
```

profile of v0, /device:TPU:248, one launch (start us, length us, event | category | flops | bytes accessed | tf_op | source)
XLA Modules:
  0.0 993.8 jit_solution(9093377417701961407)
XLA Ops:
  7.2 1.6 copy.332
  8.8 4.3 all-to-all-start.4
  14.0 4.9 all-to-all-done.4
  18.9 8.2 all_to_all.134
  27.8 1.5 copy.334
  29.3 3.3 all-to-all-start
  34.2 1.0 dynamic-slice_select_fusion
  35.6 2.8 all-to-all-done
  38.4 3.3 all-to-all-start.2
  41.8 5.6 all-to-all-done.2
  47.5 3.5 all-to-all-start.6
  52.4 1.9 collective-permute-start
  54.4 1.9 collective-permute-start.1
  56.3 1.7 compare_and_fusion
  58.0 2.7 collective-permute-done
  60.7 6.2 collective-permute-start.2
  66.9 3.7 collective-permute-start.3
  70.8 7.1 collective-permute-start.4
  77.9 5.8 collective-permute-start.5
  87.6 1.9 collective-permute-start.6
  89.5 6.5 collective-permute-start.7
  96.1 4.4 all-to-all-start.1
  101.3 9.7 all-to-all-done.1
  111.4 1.4 multiply_subtract_fusion
  112.7 1.1 copy-done
  113.9 1.1 multiply_reduce_fusion
  115.3 3.2 multiply_convert_fusion
  119.0 2.5 conditional.7
  119.0 1.9 fusion
  121.6 2.8 conditional.8
  121.6 1.9 fusion.12
  124.4 2.9 conditional.9
  124.6 1.8 fusion.25
  127.4 3.7 conditional.10
  127.4 1.9 fusion.38
  129.3 1.8 fusion.40
  131.1 1.2 copy.214
  132.5 214.7 %all-gather.2.cloned.1.call-done = bf16[12288,512]{1,0:T(8,128)(2,1)} async-done(((bf16[192,512]{1,0:T(8,128)(2,1)}), bf16[12288,512]{1,0:T(8,128)(2,1)}) %all-gather.2.cloned.1.call-update) | async-done | bytes 12582928 | tf_op jit(solution)/shard_map/all_gather | solution.py:29
  347.2 10.1 %fusion.100 = (bf16[12288,256]{1,0:T(8,128)(2,1)}, bf16[12288,256]{1,0:T(8,128)(2,1)}) fusion(bf16[12288,512]{1,0:T(8,128)(2,1)} %all-gather.2.cloned.1.call-done), kind=kLoop, calls=%fused_computation.170 | loop fusion | bytes 25165824 | tf_op jit(solution)/shard_map/slice | solution.py:31
  357.3 8.6 copy.211
  365.9 8.6 copy.215
  374.5 8.6 copy.212
  383.2 8.6 copy.216
  392.0 561.6 %while.23 = (s32[]{:T(128)}, f32[2,5,96]{2,1,0:T(8,128)S(1)}, f32[2,5,96]{2,1,0:T(8,128)S(1)}, f32[96,2,5,128]{3,0,2,1:T(8,128)S(1)}, f32[2,5,96]{2,1,0:T(8,128)...) while((s32[]{:T(128)}, f32[2,5,96]{2,1,0:T(8,128)S(1)}, ...), condition=%wide.region_33.34_spmd, body=%wide.region_22.33_spmd.sunk | while | flops 96564864 | bytes 5262439 | solution.py:235
  704.3 0.9 conditional.15
  708.3 0.9 conditional.15
  716.1 0.9 conditional.15
  727.9 0.9 conditional.15
  731.8 0.9 conditional.15
  739.7 0.9 conditional.15
  751.5 0.9 conditional.15
  755.4 0.9 conditional.15
  763.3 0.9 conditional.15
  779.0 0.9 conditional.15
  834.1 0.9 conditional.15
  845.8 0.9 conditional.15
  897.0 0.9 conditional.15
  954.2 2.2 collective-permute-start.9
  957.1 1.3 all_to_all.107
  958.4 4.3 all-to-all-start.3
  963.2 1.0 copy.221
  964.2 8.5 all-to-all-done.3
  972.7 3.5 all-to-all-start.7
  977.0 9.1 all-to-all-done.7
  (1883 shorter events, 561.1 us)
Async XLA Ops:
  7.2 25.5 %copy-start.2 = (bf16[48,5120]{1,0:T(8,128)(2,1)S(1)}, bf16[48,5120]{1,0:T(8,128)(2,1)}, u32[]{:S(2)}) copy-start(bf16[48,5120]{1,0:T(8,128)(2,1)} %param.27) | copy-start | bytes 1474564
  7.2 26.3 %copy-start.12 = (bf16[48,1024]{1,0:T(8,128)(2,1)S(1)}, bf16[48,1024]{1,0:T(8,128)(2,1)}, u32[]{:S(2)}) copy-start(bf16[48,1024]{1,0:T(8,128)(2,1)} %param.25) | copy-start | bytes 294916
  8.8 10.1 %all-to-all-start.4 = ((bf16[48,4,256]{2,0,1:T(8,128)(2,1)}), bf16[48,4,256]{2,0,1:T(8,128)(2,1)S(1)}, u32[]{:S(2)}, u32[]{:S(2)}) async-start(bf16[48,4,256]{2,0,1:T(8,128)(2,1)} %bitcast.158), calls=%async_computation.4 | async-start | bytes 196608 | tf_op jit(solution)/shard_map/all_to_all | solution.py:123
  13.1 334.1 %all-gather.2.cloned.1.call-start = ((), (), s32[]{:S(2)}) async-start(), calls=%async_computation.8 | async-start | bytes 12779520 | tf_op jit(solution)/shard_map/all_gather | solution.py:29
  29.3 9.1 all-to-all-start
  34.1 49.6 %copy-start.17 = (s32[192]{0:T(256)}, s32[192]{0:T(256)S(1)}, u32[]{:S(2)}) copy-start(s32[192]{0:T(256)S(1)} %iota_add_fusion.3) | copy-start | bytes 2308
  35.6 16.9 %copy-start.1 = (f32[192,64]{1,0:T(8,128)}, f32[192,64]{1,0:T(8,128)S(1)}, u32[]{:S(2)}) copy-start(f32[192,64]{1,0:T(8,128)S(1)} %get-tuple-element.776) | copy-start | bytes 147460
  38.4 9.1 all-to-all-start.2
  41.8 41.9 %copy-start.3 = (bf16[48,5120]{1,0:T(8,128)(2,1)S(1)}, bf16[48,5120]{1,0:T(8,128)(2,1)}, u32[]{:S(2)}) copy-start(bf16[48,5120]{1,0:T(8,128)(2,1)} %param.23) | copy-start | bytes 1474564
  47.5 48.6 %all-to-all-start.6 = ((bf16[48,4,1280]{2,0,1:T(8,128)(2,1)}), bf16[48,4,1280]{2,0,1:T(8,128)(2,1)S(1)}, u32[]{:S(2)}, u32[]{:S(2)}) async-start(bf16[48,4,1280]{2,0,1:T(8,128)(2,1)} %bitcast.155), calls=%async_computation.6 | async-start | bytes 983040 | tf_op jit(solution)/shard_map/all_to_all | solution.py:122
  51.0 45.1 %copy-start.4 = (bf16[192,2,128]{2,1,0:T(2,128)(2,1)}, bf16[192,2,128]{2,1,0:T(2,128)(2,1)S(1)}, u32[]{:S(2)}) copy-start(bf16[192,2,128]{2,1,0:T(2,128)(2,1)S(1)} %reshape.237) | copy-start | bytes 294916
  52.4 43.6 %copy-start.10 = (bf16[192,2,128]{2,1,0:T(2,128)(2,1)}, bf16[192,2,128]{2,1,0:T(2,128)(2,1)S(1)}, u32[]{:S(2)}) copy-start(bf16[192,2,128]{2,1,0:T(2,128)(2,1)S(1)} %multiply_convert_fusion.1) | copy-start | bytes 294916
  52.4 8.3 collective-permute-start
  54.4 12.6 %collective-permute-start.1 = (bf16[192,2,128]{2,1,0:T(2,128)(2,1)S(1)}, bf16[192,2,128]{2,1,0:T(2,128)(2,1)S(1)}, u32[]{:S(2)}, u32[]{:S(2)}) collective-permute-start(bf16[192,2,128]{2,1,0:T(2,128)(2,1)S(1)} %reshape.237), channel_id=1, source_target_pairs={{0,4},{4,8},{8,12},{12,16},{16,20},{20,24},{24,28},{28,32},{32,36}... | collective-permute-start | bytes 294920 | tf_op jit(solution)/shard_map/ppermute | solution.py:20
  60.7 40.5 %copy-start.18 = (bf16[192,2,128]{2,1,0:T(2,128)(2,1)}, bf16[192,2,128]{2,1,0:T(2,128)(2,1)S(1)}, u32[]{:S(2)}) copy-start(bf16[192,2,128]{2,1,0:T(2,128)(2,1)S(1)} %collective-permute-done) | copy-start | bytes 294916
  60.7 10.0 %collective-permute-start.2 = (bf16[192,2,128]{2,1,0:T(2,128)(2,1)S(1)}, bf16[192,2,128]{2,1,0:T(2,128)(2,1)S(1)}, u32[]{:S(2)}, u32[]{:S(2)}) collective-permute-start(bf16[192,2,128]{2,1,0:T(2,128)(2,1)S(1)} %collective-permute-done), channel_id=1, source_target_pairs={{0,4},{4,8},{8,12},{12,16},{16,20},{20,24},{24,28},{28,32},{32,36}... | collective-permute-start | bytes 294920 | tf_op jit(solution)/shard_map/ppermute | solution.py:20
  66.9 29.1 %copy-start.13 = (bf16[192,2,128]{2,1,0:T(2,128)(2,1)}, bf16[192,2,128]{2,1,0:T(2,128)(2,1)S(1)}, u32[]{:S(2)}) copy-start(bf16[192,2,128]{2,1,0:T(2,128)(2,1)S(1)} %collective-permute-done.1) | copy-start | bytes 294916
  66.9 11.0 %collective-permute-start.3 = (bf16[192,2,128]{2,1,0:T(2,128)(2,1)S(1)}, bf16[192,2,128]{2,1,0:T(2,128)(2,1)S(1)}, u32[]{:S(2)}, u32[]{:S(2)}) collective-permute-start(bf16[192,2,128]{2,1,0:T(2,128)(2,1)S(1)} %collective-permute-done.1), channel_id=1, source_target_pairs={{0,4},{4,8},{8,12},{12,16},{16,20},{20,24},{24,28},{28,32},{32,36}... | collective-permute-start | bytes 294920 | tf_op jit(solution)/shard_map/ppermute | solution.py:20
  70.8 40.3 %copy-start.20 = (bf16[192,2,128]{2,1,0:T(2,128)(2,1)}, bf16[192,2,128]{2,1,0:T(2,128)(2,1)S(1)}, u32[]{:S(2)}) copy-start(bf16[192,2,128]{2,1,0:T(2,128)(2,1)S(1)} %collective-permute-done.2) | copy-start | bytes 294916
  70.8 16.8 %collective-permute-start.4 = (bf16[192,2,128]{2,1,0:T(2,128)(2,1)S(1)}, bf16[192,2,128]{2,1,0:T(2,128)(2,1)}, u32[]{:S(2)}, u32[]{:S(2)}) collective-permute-start(bf16[192,2,128]{2,1,0:T(2,128)(2,1)S(1)} %collective-permute-done.2), channel_id=1, source_target_pairs={{0,4},{4,8},{8,12},{12,16},{16,20},{20,24},{24,28},{28,32},{32,36}... | collective-permute-start | bytes 294920 | tf_op jit(solution)/shard_map/ppermute | solution.py:20
  77.9 18.2 %copy-start.15 = (bf16[192,2,128]{2,1,0:T(2,128)(2,1)}, bf16[192,2,128]{2,1,0:T(2,128)(2,1)S(1)}, u32[]{:S(2)}) copy-start(bf16[192,2,128]{2,1,0:T(2,128)(2,1)S(1)} %collective-permute-done.3) | copy-start | bytes 294916
  77.9 11.6 %collective-permute-start.5 = (bf16[192,2,128]{2,1,0:T(2,128)(2,1)S(1)}, bf16[192,2,128]{2,1,0:T(2,128)(2,1)}, u32[]{:S(2)}, u32[]{:S(2)}) collective-permute-start(bf16[192,2,128]{2,1,0:T(2,128)(2,1)S(1)} %collective-permute-done.3), channel_id=1, source_target_pairs={{0,4},{4,8},{8,12},{12,16},{16,20},{20,24},{24,28},{28,32},{32,36}... | collective-permute-start | bytes 294920 | tf_op jit(solution)/shard_map/ppermute | solution.py:20
  87.6 43.5 %collective-permute-start.6 = (bf16[192,2,128]{2,1,0:T(2,128)(2,1)}, bf16[192,2,128]{2,1,0:T(2,128)(2,1)}, u32[]{:S(2)}, u32[]{:S(2)}) collective-permute-start(bf16[192,2,128]{2,1,0:T(2,128)(2,1)} %collective-permute-done.4), channel_id=1, source_target_pairs={{0,4},{4,8},{8,12},{12,16},{16,20},{20,24},{24,28},{28,32},{32,36}... | collective-permute-start | bytes 294920 | tf_op jit(solution)/shard_map/ppermute | solution.py:20
  89.5 41.6 %collective-permute-start.7 = (bf16[192,2,128]{2,1,0:T(2,128)(2,1)}, bf16[192,2,128]{2,1,0:T(2,128)(2,1)}, u32[]{:S(2)}, u32[]{:S(2)}) collective-permute-start(bf16[192,2,128]{2,1,0:T(2,128)(2,1)} %collective-permute-done.5), channel_id=1, source_target_pairs={{0,4},{4,8},{8,12},{12,16},{16,20},{20,24},{24,28},{28,32},{32,36}... | collective-permute-start | bytes 294920 | tf_op jit(solution)/shard_map/ppermute | solution.py:20
  96.1 14.9 %all-to-all-start.1 = ((bf16[48,4,1280]{2,0,1:T(8,128)(2,1)}), bf16[48,4,1280]{2,0,1:T(8,128)(2,1)S(1)}, u32[]{:S(2)}, u32[]{:S(2)}) async-start(bf16[48,4,1280]{2,0,1:T(8,128)(2,1)} %bitcast.156), calls=%async_computation.1 | async-start | bytes 983040 | tf_op jit(solution)/shard_map/all_to_all | solution.py:119
  101.3 29.9 %collective-permute-start.8 = (bf16[96,1280]{1,0:T(8,128)(2,1)}, bf16[96,1280]{1,0:T(8,128)(2,1)}, u32[]{:S(2)}, u32[]{:S(2)}) collective-permute-start(bf16[96,1280]{1,0:T(8,128)(2,1)} %bitcast.46), channel_id=1, source_target_pairs={{0,128},{4,132},{8,136},{12,140},{16,144},{20,148},{24,152},{28,15... | collective-permute-start | bytes 737288 | tf_op jit(solution)/shard_map/ppermute | solution.py:24
  112.7 1.1 copy-start
  115.3 3.6 copy-start.5
  115.3 3.6 copy-start.9
  115.3 3.6 copy-start.11
  119.0 2.6 copy-start.8
  119.0 2.6 copy-start.14
  119.0 2.6 copy-start.19
  121.6 2.8 copy-start.7
  121.6 2.8 copy-start.16
  121.6 2.8 copy-start.21
  124.4 2.9 copy-start.6
  383.2 8.8 slice-start
  954.2 8.7 collective-permute-start.9
  958.4 14.3 %all-to-all-start.3 = ((bf16[4,48,1280]{2,1,0:T(8,128)(2,1)}), bf16[4,48,1280]{2,1,0:T(8,128)(2,1)S(1)}, u32[]{:S(2)}, u32[]{:S(2)}) async-start(bf16[4,48,1280]{2,1,0:T(8,128)(2,1)} %all_to_all.107), calls=%async_computation.3 | async-start | bytes 983040 | tf_op jit(solution)/shard_map/all_to_all | solution.py:247
  972.7 13.4 %all-to-all-start.7 = ((bf16[4,48,1280]{2,1,0:T(8,128)(2,1)}), bf16[4,48,1280]{2,1,0:T(8,128)(2,1)S(1)}, u32[]{:S(2)}, u32[]{:S(2)}) async-start(bf16[4,48,1280]{2,1,0:T(8,128)(2,1)} %bitcast.52), calls=%async_computation.7 | async-start | bytes 983040 | tf_op jit(solution)/shard_map/all_to_all | solution.py:248
Sparse Core Ops, SparseCore 0:
  27.9 319.2 all-gather.1
where the time goes:
time: 1010 us; the launch traced here: 994 us
  waiting for transfers between devices  258 us (26%)
  loops' own time  183 us (18%)
  local copies, waits for them, and re-layouts  177 us (18%)
  matrix products  154 us (15%)
  other arithmetic  131 us (13%)
  starting transfers between devices  63.8 us (6%)
  between operations  17.9 us (2%)
    all_gather x1, waiting for transfers between devices, in_one_piece(): lax.all_gather(both, axis, axis=dim, tiled=True)  215 us
    another operation x1, loops' own time, shards(): lax.fori_loop(0, piece_rows // half_rows, advance, (initial, initial))  172 us
    dynamic_slice x128, local copies, waits for them, and re-layouts, advance(): lax.dynamic_slice_in_dim(value_piece, anchor, half_rows, 0)  106 us
    reduce_or x128, other arithmetic, global_update(): return lax.cond(jnp.any(allowed), update, lambda carried: carried, running)  92.8 us
    dot_general x195, matrix products, update(): jnp.einsum('hgqk,khd->qhgd', weights.astype(jnp.bfloat16), value_block, p...  88.7 us
    dot_general x195, matrix products, update(): jnp.einsum('qhgd,khd->hgqk', queries, key_block, preferred_element_type=j...  65.6 us
    ppermute x8, starting transfers between devices, passed_along(): return lax.ppermute(shard, axis, pairs)  35 us
    slice x3, local copies, waits for them, and re-layouts, in_one_piece(): lax.slice_in_dim(result, at, at + a.shape[along], axis=along)  27.3 us
  transfers between devices with their start and end apart: 18, of which 8 were waited for; matrix products, arithmetic and copies ran while one was open for 3% of the time, Pallas kernels for 0%

commit v1 on v0

v1 whole, which is shorter than its diff:
```python
import functools

import jax
import jax.numpy as jnp
from jax import lax
from jax.experimental import pallas as pl
from jax.experimental.pallas import tpu as pltpu
from jax.sharding import PartitionSpec as P

HEAD = 128
GROUP = 5
WIDE = GROUP * HEAD
TOK = 192
OWN = 48
NZ, NY = 8, 4
ROWS = GROUP * TOK
CHUNK = NY * TOK
SPAN = 4
KEYS = (SPAN + 1) * TOK
TILE = 320

rope_base = 500000.0
norm_epsilon = 1e-06
temper_shift = 13
temper_slope = 0.1
masked_score = -1e30
log2e = 1.4426950408889634
scaling = HEAD ** (-0.5)

MESH = pl.DeviceIdType.MESH
KG, VG, KL, VL, QL, QG, OL, OG = range(8)


def tiled(x, n):
    return jnp.concatenate([x] * n, axis=1)


def kernel(
    ql_ref, kl_ref, vl_hbm, qg_hbm, kg_hbm, vg_hbm, cos_ref, sin_ref, kid_ref, qid_ref,
    ol_hbm, og_hbm,
    kv, lkv, qg_buf, lq_buf, nq, nk, qs, m_ref, acc, og_buf, ol_buf, bias,
    a2a_send, a2a_recv, ring_send, ring_recv, halo_send, halo_recv,
):
    ctx = lax.axis_index("ctx")
    head = lax.axis_index("head")
    x_lo = ctx // 32
    c = ctx % 32
    z = c // NY
    y = c % NY
    g = x_lo * 4 + head
    flip = 31 - c

    def at(row, member):
        return {"ctx": (member // 4) * 32 + row, "head": member % 4}

    def line(row):
        return {"ctx": x_lo * 32 + row, "head": head}

    def wrap(v, n):
        return lax.rem(v + n, n)

    barrier = pltpu.get_barrier_semaphore()

    def greet(device):
        pl.semaphore_signal(barrier, inc=1, device_id=device, device_id_type=MESH)

    @pl.loop(0, 8)
    def _(t):
        greet(at(flip, t))

    @pl.loop(1, 8)
    def _(t):
        greet(at(c, g ^ t))

    for s in (1, -1):
        greet(line(z * NY + wrap(y + s, NY)))
        greet(line(wrap(z + s, NZ) * NY + y))

    @pl.loop(1, SPAN + 1)
    def _(t):
        greet(line(lax.rem(c + t, 32)))
        greet(line(lax.rem(c - t + 32, 32)))

    pl.semaphore_wait(barrier, 27)

    my_rows = pl.ds(head * OWN, OWN)

    def exchange_refs(kind, target):
        narrow = pl.ds(pl.multiple_of(target * HEAD, HEAD), HEAD)
        wide = pl.ds(pl.multiple_of(target * WIDE, HEAD), WIDE)
        mine = pl.ds(pl.multiple_of(g * WIDE, HEAD), WIDE)
        their = pl.ds(lax.rem(target, 4) * OWN, OWN)
        if kind == KG:
            return kg_hbm.at[:, narrow], kv.at[x_lo, z, y, 0, my_rows, :]
        if kind == VG:
            return vg_hbm.at[:, narrow], kv.at[x_lo, z, y, 1, my_rows, :]
        if kind == KL:
            return nk.at[:, narrow], lkv.at[x_lo, SPAN, 0, my_rows, :]
        if kind == VL:
            return vl_hbm.at[:, narrow], lkv.at[x_lo, SPAN, 1, my_rows, :]
        if kind == QL:
            return nq.at[:, wide], lq_buf.at[x_lo, my_rows, :]
        if kind == QG:
            return qg_hbm.at[:, wide], qg_buf.at[x_lo, my_rows, :]
        if kind == OL:
            return ol_buf.at[target // 4, their, :], ol_hbm.at[:, mine]
        return og_buf.at[target // 4, their, :], og_hbm.at[:, mine]

    def exchange(kind, d):
        target = g ^ d
        src, dst = exchange_refs(kind, target)
        if kind == QG:
            row = jnp.where(x_lo == 0, c, flip)
        elif kind == OG:
            row = jnp.where(target < 4, c, flip)
        else:
            row = c
        return pltpu.make_async_remote_copy(
            src_ref=src,
            dst_ref=dst,
            send_sem=a2a_send.at[kind, d],
            recv_sem=a2a_recv.at[kind, g],
            device_id=at(row, target),
            device_id_type=MESH,
        )

    def exchange_own(kind):
        src, dst = exchange_refs(kind, g)
        return pltpu.make_async_copy(src, dst, a2a_recv.at[kind, g])

    def send(kind):
        if kind in (QG, OG):

            @pl.when(x_lo == 0)
            def _():
                exchange_own(kind).start()

            @pl.when(x_lo == 1)
            def _():
                exchange(kind, 0).start()
        else:
            exchange_own(kind).start()

        @pl.loop(1, 8)
        def _(d):
            exchange(kind, d).start()

    def sent(kind):
        if kind in (QG, OG):

            @pl.when(x_lo == 1)
            def _():
                exchange(kind, 0).wait_send()

        @pl.loop(1, 8)
        def _(d):
            exchange(kind, d).wait_send()

    def received(kind):
        @pl.loop(0, 8)
        def _(t):
            _, dst = exchange_refs(kind, g)
            pltpu.make_async_copy(dst, dst, a2a_recv.at[kind, t]).wait()

    def hop(number, ref, device):
        return pltpu.make_async_remote_copy(
            src_ref=ref,
            dst_ref=ref,
            send_sem=ring_send.at[number],
            recv_sem=ring_recv.at[number],
            device_id=device,
            device_id_type=MESH,
        )

    def y_next(s):
        return line(z * NY + wrap(y + s, NY))

    def z_next(s):
        return line(wrap(z + s, NZ) * NY + y)

    def early_y(step, s):
        if step == 1:
            ref = kv.at[0, z, y]
        else:
            ref = kv.at[0, z, wrap(y - s, NY), 0 if s == 1 else 1]
        return hop(2 * (step - 1) + (s == 1), ref, y_next(s))

    def early_z(step, s):
        chunk = wrap(z - s * (step - 1), NZ)
        if step < 4:
            ref = kv.at[0, chunk]
        else:
            ref = kv.at[0, chunk, :, 0 if s == 1 else 1]
        return hop(4 + 2 * (step - 1) + (s == 1), ref, z_next(s))

    def late_z(step, s):
        chunk = wrap(z - s * (step - 1), NZ)
        if step < 4:
            ref = kv.at[1, chunk, y]
        else:
            ref = kv.at[1, chunk, y, 0 if s == 1 else 1]
        return hop(12 + 2 * (step - 1) + (s == 1), ref, z_next(s))

    def late_y(step, s):
        if step == 1:
            ref = kv.at[1, :, y]
        else:
            ref = kv.at[1, :, wrap(y - s, NY), 0 if s == 1 else 1]
        return hop(20 + 2 * (step - 1) + (s == 1), ref, y_next(s))

    def begin(family, step):
        for s in (1, -1):
            family(step, s).start()

    def arrived(family, step):
        for s in (1, -1):
            family(step, s).wait_recv()

    def left(family, steps):
        for step in range(1, steps + 1):
            for s in (1, -1):
                family(step, s).wait_send()

    def halo(d, e):
        row = lax.rem(c + d, 32)
        other = jnp.where(c + d >= 32, 1 - e, e)
        return pltpu.make_async_remote_copy(
            src_ref=lkv.at[e, SPAN],
            dst_ref=lkv.at[other, SPAN - d],
            send_sem=halo_send.at[d - 1, e],
            recv_sem=halo_recv.at[d - 1, other],
            device_id=line(row),
            device_id_type=MESH,
        )

    def normalized(x):
        x = x.astype(jnp.float32)
        r = x * cos_ref[...] + pltpu.roll(x, HEAD // 2, 1) * sin_ref[...]
        mean = jnp.mean(r * r, axis=-1, keepdims=True)
        return (r * lax.rsqrt(mean + norm_epsilon)).astype(jnp.bfloat16)

    send(KG)
    send(VG)
    for h in range(8):
        cols = slice(h * HEAD, (h + 1) * HEAD)
        nk[:, cols] = normalized(kl_ref[:, cols])
    received(KG)
    received(VG)
    begin(late_z, 1)
    begin(early_y, 1)
    send(KL)
    send(VL)
    send(QG)

    @pl.loop(0, 8)
    def _(t):
        for h in range(GROUP):
            cols = pl.ds(pl.multiple_of(t * WIDE + h * HEAD, HEAD), HEAD)
            nq[:, cols] = normalized(ql_ref[:, cols])

    send(QL)
    arrived(early_y, 1)
    begin(early_y, 2)
    arrived(late_z, 1)
    begin(late_z, 2)
    received(KL)
    received(VL)

    @pl.loop(1, SPAN + 1)
    def _(d):
        halo(d, 0).start()
        halo(d, 1).start()

    arrived(early_y, 2)
    begin(early_z, 1)
    arrived(late_z, 2)
    begin(late_z, 3)

    received(QG)
    m_ref[...] = jnp.full(m_ref.shape, masked_score, jnp.float32)
    acc[...] = jnp.zeros(acc.shape, jnp.float32)

    @pl.loop(0, 2)
    def _(e):
        block = jnp.where(e == 0, c, 63 - c)
        pos = block * TOK + lax.broadcasted_iota(jnp.int32, (TOK, HEAD), 0)
        level = lax.shift_right_logical(pos + 1, temper_shift) + 1
        temper = 1.0 + temper_slope * jnp.log(level.astype(jnp.float32))
        factor = temper * (scaling * log2e)
        for h in range(GROUP):
            x = qg_buf[e, :, h * HEAD : (h + 1) * HEAD].astype(jnp.float32) * factor
            high = x.astype(jnp.bfloat16)
            low = (x - high.astype(jnp.float32)).astype(jnp.bfloat16)
            qs[e, h * TOK : (h + 1) * TOK, :] = jnp.concatenate([high, low], axis=1)

    arrived(late_z, 3)
    begin(late_z, 4)

    received(QL)

    @pl.loop(1, SPAN + 1)
    def _(d):
        halo(d, 0).wait_recv()
        halo(d, 1).wait_recv()

    arrived(late_z, 4)
    begin(late_y, 1)

    @pl.loop(0, 2)
    def _(e):
        block = e * 32 + c
        row_pos = lax.broadcasted_iota(jnp.int32, (TOK, KEYS), 0) + SPAN * TOK
        key_pos = lax.broadcasted_iota(jnp.int32, (TOK, KEYS), 1)
        allowed = (qid_ref[e] == kid_ref[e]) & (key_pos <= row_pos)
        bias[...] = jnp.where(allowed, 0.0, masked_score)
        k = lkv[e, :, 0].reshape(KEYS, HEAD)
        v = lkv[e, :, 1].reshape(KEYS, HEAD)
        va = jnp.concatenate([v, jnp.ones((KEYS, HEAD), jnp.bfloat16)], axis=1)
        for h in range(GROUP):
            cols = slice(h * HEAD, (h + 1) * HEAD)
            s = lax.dot_general(
                lq_buf[e, :, cols], k, (((1,), (1,)), ((), ())),
                preferred_element_type=jnp.float32,
            )
            p = jnp.exp2(s * (scaling * log2e) + bias[...]).astype(jnp.bfloat16)
            o = jnp.dot(p, va, preferred_element_type=jnp.float32)
            ol_buf[e, :, cols] = (o[:, :HEAD] / o[:, HEAD:]).astype(jnp.bfloat16)

    send(OL)

    def unit(eq, ek, chunk, offset=None):
        k = kv[ek, chunk, :, 0].reshape(CHUNK, HEAD)
        v = kv[ek, chunk, :, 1].reshape(CHUNK, HEAD)
        kk = jnp.concatenate([k, k], axis=1)
        va = jnp.concatenate([v, jnp.ones((CHUNK, HEAD), jnp.bfloat16)], axis=1)
        for t in range(ROWS // TILE):
            rows = pl.ds(t * TILE, TILE)
            s = lax.dot_general(
                qs[eq, rows, :], kk, (((1,), (1,)), ((), ())),
                preferred_element_type=jnp.float32,
            )
            if offset is not None:
                r = t * TILE + lax.broadcasted_iota(jnp.int32, (TILE, HEAD), 0)
                for h in range(GROUP - 1, 0, -1):
                    r = jnp.where(r >= h * TOK, r - h * TOK, r)
                limit = tiled(r + offset, CHUNK // HEAD)
                key = lax.broadcasted_iota(jnp.int32, (TILE, CHUNK), 1)
                s = jnp.where(key <= limit, s, masked_score)
            before = m_ref[eq, rows, :]
            peak = jnp.maximum(before, jnp.max(s, axis=1, keepdims=True))
            factor = jnp.exp2(before - peak)
            p = jnp.exp2(s - tiled(peak, CHUNK // HEAD)).astype(jnp.bfloat16)
            acc[eq, rows, :] = acc[eq, rows, :] * tiled(factor, 2) + jnp.dot(
                p, va, preferred_element_type=jnp.float32
            )
            m_ref[eq, rows, :] = peak

    @pl.loop(0, 24)
    def _(j):
        @pl.when(j == 2)
        def _():
            arrived(early_z, 1)
            begin(early_z, 2)

        @pl.when(j == 6)
        def _():
            arrived(early_z, 2)
            begin(early_z, 3)

        @pl.when(j == 10)
        def _():
            arrived(early_z, 3)
            begin(early_z, 4)
            arrived(late_y, 1)
            begin(late_y, 2)

        @pl.when(j == 14)
        def _():
            arrived(early_z, 4)

        @pl.when(j == 16)
        def _():
            arrived(late_y, 2)

        i = j // 2
        away = (i + 1) // 2
        near = lax.rem(z + jnp.where(lax.rem(i, 2) == 1, 8 - away, away), NZ)
        late_keys = j >= 16
        chunk = jnp.where(late_keys, j - 16, near)
        eq = jnp.where(late_keys | (lax.rem(j, 2) == 0), 1, 0)
        ek = jnp.where(late_keys, 1, 0)
        do = jnp.where(late_keys, chunk < 7 - z, (eq == 1) | (chunk < z))

        @pl.when(do)
        def _():
            unit(eq, ek, chunk)

    @pl.loop(0, 2)
    def _(e):
        unit(e, e, jnp.where(e == 0, z, 7 - z), TOK * jnp.where(e == 0, y, 3 - y))
        for h in range(GROUP):
            o = acc[e, h * TOK : (h + 1) * TOK, :]
            og_buf[e, :, h * HEAD : (h + 1) * HEAD] = (o[:, :HEAD] / o[:, HEAD:]).astype(
                jnp.bfloat16
            )

    send(OG)
    for kind in (KG, VG, KL, VL, QL, QG, OL):
        sent(kind)
    left(early_y, 2)
    left(early_z, 4)
    left(late_z, 4)
    left(late_y, 2)

    @pl.loop(1, SPAN + 1)
    def _(d):
        halo(d, 0).wait_send()
        halo(d, 1).wait_send()

    received(OL)
    received(OG)
    sent(OG)


def shards(
    query_local, key_local, value_local, stretch_labels, query_global, key_global, value_global
):
    ctx = lax.axis_index("ctx")
    head = lax.axis_index("head")
    c = ctx % 32
    positions = (ctx * TOK + head * OWN + jnp.arange(OWN, dtype=jnp.int32)).astype(jnp.float32)
    half = HEAD // 2
    frequency = rope_base ** (-(jnp.arange(half, dtype=jnp.float32) * 2.0 / HEAD))
    angles = positions[:, None] * frequency[None, :]
    cosine, sine = jnp.cos(angles), jnp.sin(angles)
    cosine = jnp.concatenate([cosine, cosine], axis=1)
    sine = jnp.concatenate([-sine, sine], axis=1)
    padded = jnp.concatenate([jnp.full((SPAN * TOK,), -1, jnp.int32), stretch_labels])
    kid = jnp.stack(
        [lax.dynamic_slice_in_dim(padded, (32 * e + c) * TOK, KEYS, 0) for e in range(2)]
    )
    qid = kid[:, SPAN * TOK :].reshape(2, TOK, 1)
    kid = kid.reshape(2, 1, KEYS)
    any_space = pl.BlockSpec(memory_space=pl.ANY)
    vmem = pl.BlockSpec(memory_space=pltpu.VMEM)
    bf16, f32 = jnp.bfloat16, jnp.float32
    out = jax.ShapeDtypeStruct(query_local.shape, bf16)
    return pl.pallas_call(
        kernel,
        out_shape=(out, out),
        in_specs=[vmem, vmem] + [any_space] * 4 + [vmem] * 4,
        out_specs=(any_space, any_space),
        scratch_shapes=[
            pltpu.VMEM((2, NZ, NY, 2, TOK, HEAD), bf16),
            pltpu.VMEM((2, SPAN + 1, 2, TOK, HEAD), bf16),
            pltpu.VMEM((2, TOK, WIDE), bf16),
            pltpu.VMEM((2, TOK, WIDE), bf16),
            pltpu.VMEM((OWN, 8 * WIDE), bf16),
            pltpu.VMEM((OWN, 8 * HEAD), bf16),
            pltpu.VMEM((2, ROWS, 2 * HEAD), bf16),
            pltpu.VMEM((2, ROWS, HEAD), f32),
            pltpu.VMEM((2, ROWS, 2 * HEAD), f32),
            pltpu.VMEM((2, TOK, WIDE), bf16),
            pltpu.VMEM((2, TOK, WIDE), bf16),
            pltpu.VMEM((TOK, KEYS), f32),
            pltpu.SemaphoreType.DMA((8, 8)),
            pltpu.SemaphoreType.DMA((8, 8)),
            pltpu.SemaphoreType.DMA((24,)),
            pltpu.SemaphoreType.DMA((24,)),
            pltpu.SemaphoreType.DMA((SPAN, 2)),
            pltpu.SemaphoreType.DMA((SPAN, 2)),
        ],
        compiler_params=pltpu.CompilerParams(
            collective_id=0, has_side_effects=True, vmem_limit_bytes=48 << 20
        ),
    )(
        query_local, key_local, value_local, query_global, key_global, value_global,
        cosine, sine, kid, qid,
    )


def solution(mesh):
    rows = P(("ctx", "head"), None)
    return jax.shard_map(
        shards,
        mesh=mesh,
        in_specs=(rows, rows, rows, P(), rows, rows, rows),
        out_specs=(rows, rows),
        check_vma=False,
    )
```

time: 1010 us -> 143 us (0.14)
  the two profiles are of different devices: /device:TPU:248 before, /device:TPU:1 now
where the time goes in v1:
time: 143 us; the launch traced here: 142 us
  Pallas kernels  134 us (94%)
  local copies, waits for them, and re-layouts  7.12 us (5%)
    pallas_call x1, Pallas kernels, shards(): pl.pallas_call(kernel, out_shape=(out, out), in_specs=[vmem, vmem] + [any...  134 us
    unnamed x16, local copies, waits for them, and re-layouts  6.89 us

profile of v1, /device:TPU:1, one launch (start us, length us, event | category | flops | bytes accessed | tf_op | source)
XLA Modules:
  0.0 142.4 jit_solution(2992130148656070353)
XLA Ops:
  0.6 0.0 copy-start.6
  0.6 0.0 copy-start
  0.7 0.7 copy-done.6
  1.4 0.1 pad_dynamic-slice_fusion.1
  1.6 0.2 fusion
  1.7 0.1 pad_maximum_fusion
  1.8 0.1 copy.10.qid_ref
  2.0 0.0 copy-done
  2.0 0.0 copy-start.1
  2.0 1.0 copy-done.1
  3.0 0.0 copy-start.2
  3.0 0.9 copy-done.2
  3.9 0.0 copy-start.3
  3.9 0.9 copy-done.3
  4.8 0.0 copy-start.4
  4.8 0.9 copy-done.4
  5.7 0.0 copy-start.5
  5.7 0.9 copy-done.5
  6.6 134.3 %shard_map.86 = (bf16[48,5120]{1,0:T(8,128)(2,1)S(1)}, bf16[48,5120]{1,0:T(8,128)(2,1)S(1)}) custom-call(bf16[48,5120]{1,0:T(8,128)(2,1)S(1)} %copy-done, bf16[48,1024]{1,0:T(8,128)(2,1)S(1)} %copy-done.2, bf16[48,1024]{1,0:T(8,128)(2,1)S(1)} %copy-done.3, bf16[48,5120]{1,0:T(8,128)(2,1)S(1)} %copy-done.1, bf16[48,1024]{1,0:T(8,128)(2,1)S(1)} %copy-done.4, ...), custom_call_target="tpu_custom_call" | custom-call | tf_op jit(solution)/shard_map/pallas_call | solution.py:448
  140.8 0.8 copy.13
  141.6 0.8 copy.14
  (5 shorter events, 0.0 us)
Async XLA Ops:
  0.6 0.8 copy-start.6
  0.6 1.3 copy-start
  2.0 1.0 copy-start.1
  3.0 0.9 copy-start.2
  3.9 0.9 copy-start.3
  4.8 0.9 copy-start.4
  5.7 0.9 copy-start.5

commit v2 on v1

v2 whole, which is shorter than its diff:
```python
import functools

import jax
import jax.numpy as jnp
from jax import lax
from jax.experimental import pallas as pl
from jax.experimental.pallas import tpu as pltpu
from jax.sharding import PartitionSpec as P

HEAD = 128
GROUP = 5
WIDE = GROUP * HEAD
TOK = 192
OWN = 48
NZ, NY = 8, 4
ROWS = GROUP * TOK
CHUNK = NY * TOK
SPAN = 4
KEYS = (SPAN + 1) * TOK
TILE = 320

rope_base = 500000.0
norm_epsilon = 1e-06
temper_shift = 13
temper_slope = 0.1
masked_score = -1e30
log2e = 1.4426950408889634
scaling = HEAD ** (-0.5)

MESH = pl.DeviceIdType.MESH
KG, VG, KL, VL, QL, QG, OL, OG = range(8)


def tiled(x, n):
    return jnp.concatenate([x] * n, axis=1)


def kernel(
    ql_hbm, kl_hbm, vl_hbm, qg_hbm, kg_hbm, vg_hbm, cos_ref, sin_ref, kid_ref, qid_ref,
    ol_hbm, og_hbm,
    ql_ref, kl_ref, kv, lkv, qg_buf, lq_buf, nq, nk, qs, m_ref, acc, og_buf, ol_buf, bias,
    a2a_send, a2a_recv, ring_send, ring_recv, halo_send, halo_recv, load_sem,
):
    ctx = lax.axis_index("ctx")
    head = lax.axis_index("head")
    x_lo = ctx // 32
    c = ctx % 32
    z = c // NY
    y = c % NY
    g = x_lo * 4 + head

    def at(row, member):
        return {"ctx": (member // 4) * 32 + row, "head": member % 4}

    def line(row):
        return {"ctx": x_lo * 32 + row, "head": head}

    def wrap(v, n):
        return lax.rem(v + n, n)

    barrier = pltpu.get_barrier_semaphore()

    def greet(device):
        pl.semaphore_signal(barrier, inc=1, device_id=device, device_id_type=MESH)

    @pl.loop(1, 8)
    def _(t):
        greet(at(c, g ^ t))

    for s in (1, -1):
        greet(line(z * NY + wrap(y + s, NY)))
        greet(line(wrap(z + s, NZ) * NY + y))

    @pl.loop(1, SPAN + 1)
    def _(t):
        greet(line(lax.rem(c + t, 32)))
        greet(line(lax.rem(c - t + 32, 32)))

    load_k = pltpu.make_async_copy(kl_hbm, kl_ref, load_sem.at[0])
    load_q = pltpu.make_async_copy(ql_hbm, ql_ref, load_sem.at[1])
    load_k.start()
    load_q.start()
    pl.semaphore_wait(barrier, 19)

    my_rows = pl.ds(head * OWN, OWN)

    def exchange_refs(kind, target):
        narrow = pl.ds(pl.multiple_of(target * HEAD, HEAD), HEAD)
        wide = pl.ds(pl.multiple_of(target * WIDE, HEAD), WIDE)
        mine = pl.ds(pl.multiple_of(g * WIDE, HEAD), WIDE)
        their = pl.ds(lax.rem(target, 4) * OWN, OWN)
        if kind == KG:
            return kg_hbm.at[:, narrow], kv.at[x_lo, z, y, 0, my_rows, :]
        if kind == VG:
            return vg_hbm.at[:, narrow], kv.at[x_lo, z, y, 1, my_rows, :]
        if kind == KL:
            return nk.at[:, narrow], lkv.at[x_lo, SPAN, 0, my_rows, :]
        if kind == VL:
            return vl_hbm.at[:, narrow], lkv.at[x_lo, SPAN, 1, my_rows, :]
        if kind == QL:
            return nq.at[:, wide], lq_buf.at[x_lo, my_rows, :]
        if kind == QG:
            return qg_hbm.at[:, wide], qg_buf.at[x_lo, my_rows, :]
        if kind == OL:
            return ol_buf.at[target // 4, their, :], ol_hbm.at[:, mine]
        return og_buf.at[target // 4, their, :], og_hbm.at[:, mine]

    def exchange(kind, d):
        target = g ^ d
        src, dst = exchange_refs(kind, target)
        return pltpu.make_async_remote_copy(
            src_ref=src,
            dst_ref=dst,
            send_sem=a2a_send.at[kind, d],
            recv_sem=a2a_recv.at[kind, g],
            device_id=at(c, target),
            device_id_type=MESH,
        )

    def exchange_own(kind):
        src, dst = exchange_refs(kind, g)
        return pltpu.make_async_copy(src, dst, a2a_recv.at[kind, g])

    def send(kind):
        exchange_own(kind).start()

        @pl.loop(1, 8)
        def _(d):
            exchange(kind, d).start()

    def send_global(e):
        @pl.loop(0, 4)
        def _(h):
            d = g ^ (4 * e + h)

            @pl.when(d == 0)
            def _():
                exchange_own(OG).start()

            @pl.when(d != 0)
            def _():
                exchange(OG, d).start()

    def sent(kind):
        @pl.loop(1, 8)
        def _(d):
            exchange(kind, d).wait_send()

    def received(kind):
        @pl.loop(0, 8)
        def _(t):
            _, dst = exchange_refs(kind, g)
            pltpu.make_async_copy(dst, dst, a2a_recv.at[kind, t]).wait()

    def hop(number, ref, device):
        return pltpu.make_async_remote_copy(
            src_ref=ref,
            dst_ref=ref,
            send_sem=ring_send.at[number],
            recv_sem=ring_recv.at[number],
            device_id=device,
            device_id_type=MESH,
        )

    def y_next(s):
        return line(z * NY + wrap(y + s, NY))

    def z_next(s):
        return line(wrap(z + s, NZ) * NY + y)

    def near(i):
        return wrap(z + (-((i + 1) // 2) if i % 2 else i // 2), NZ)

    def early_y(step, s):
        if step == 1:
            ref = kv.at[0, z, y]
        else:
            ref = kv.at[0, z, wrap(y - s, NY), 0 if s == 1 else 1]
        return hop(2 * (step - 1) + (s == 1), ref, y_next(s))

    def early_first(n, s):
        ref = kv.at[0, z, lax.rem(y + (0, 3, 1, 2)[n], NY)]
        return hop(18 + 2 * n + (s == 1), ref, z_next(s))

    def early_z(step, s):
        ref = kv.at[0, wrap(z - s * (step - 1), NZ)]
        return hop(4 + 2 * (step - 2) + (s == 1), ref, z_next(s))

    def late_z(step, s):
        ref = kv.at[1, wrap(z - s * (step - 1), NZ), y]
        return hop(10 + 2 * (step - 1) + (s == 1), ref, z_next(s))

    def late_first(i, s):
        return hop(26 + 2 * i + (s == 1), kv.at[1, near(i), y], y_next(s))

    def late_second(i, s):
        ref = kv.at[1, near(i), wrap(y - s, NY), 0 if s == 1 else 1]
        return hop(42 + 2 * i + (s == 1), ref, y_next(s))

    def ways(family, step):
        return (-1,) if family in (early_z, late_z) and step == 4 else (1, -1)

    def begin(family, *steps):
        for step in steps:
            for s in ways(family, step):
                family(step, s).start()

    def arrived(family, *steps):
        for step in steps:
            for s in ways(family, step):
                family(step, s).wait_recv()

    def left(family, *steps):
        for step in steps:
            for s in ways(family, step):
                family(step, s).wait_send()

    def halo(d, e):
        row = lax.rem(c + d, 32)
        other = jnp.where(c + d >= 32, 1 - e, e)
        return pltpu.make_async_remote_copy(
            src_ref=lkv.at[e, SPAN],
            dst_ref=lkv.at[other, SPAN - d],
            send_sem=halo_send.at[d - 1, e],
            recv_sem=halo_recv.at[d - 1, other],
            device_id=line(row),
            device_id_type=MESH,
        )

    def normalized(x):
        x = x.astype(jnp.float32)
        r = x * cos_ref[...] + pltpu.roll(x, HEAD // 2, 1) * sin_ref[...]
        mean = jnp.mean(r * r, axis=-1, keepdims=True)
        return (r * lax.rsqrt(mean + norm_epsilon)).astype(jnp.bfloat16)

    send(KG)
    send(VG)
    load_k.wait()
    for h in range(8):
        cols = slice(h * HEAD, (h + 1) * HEAD)
        nk[:, cols] = normalized(kl_ref[:, cols])
    load_q.wait()

    @pl.loop(0, 8)
    def _(t):
        for h in range(GROUP):
            cols = pl.ds(pl.multiple_of(t * WIDE + h * HEAD, HEAD), HEAD)
            nq[:, cols] = normalized(ql_ref[:, cols])

    m_ref[...] = jnp.full(m_ref.shape, masked_score, jnp.float32)
    acc[...] = jnp.zeros(acc.shape, jnp.float32)
    received(KG)
    received(VG)
    begin(late_z, 1)
    begin(early_y, 1)
    begin(early_first, 0)
    begin(late_first, 0)
    send(QG)
    arrived(early_y, 1)
    begin(early_y, 2)
    begin(early_first, 1, 2)
    arrived(late_z, 1)
    begin(late_z, 2)
    begin(late_first, 1, 2)
    arrived(early_y, 2)
    begin(early_first, 3)
    send(KL)
    send(VL)
    arrived(late_z, 2)
    begin(late_z, 3)
    begin(late_first, 3, 4)
    received(QG)

    @pl.loop(0, 2)
    def _(e):
        block = e * 32 + c
        pos = block * TOK + lax.broadcasted_iota(jnp.int32, (TOK, HEAD), 0)
        level = lax.shift_right_logical(pos + 1, temper_shift) + 1
        temper = 1.0 + temper_slope * jnp.log(level.astype(jnp.float32))
        factor = temper * (scaling * log2e)
        for h in range(GROUP):
            x = qg_buf[e, :, h * HEAD : (h + 1) * HEAD].astype(jnp.float32) * factor
            high = x.astype(jnp.bfloat16)
            low = (x - high.astype(jnp.float32)).astype(jnp.bfloat16)
            qs[e, h * TOK : (h + 1) * TOK, :] = jnp.concatenate([high, low], axis=1)

    def local_attention():
        received(QL)

        @pl.loop(1, SPAN + 1)
        def _(d):
            halo(d, 0).wait_recv()
            halo(d, 1).wait_recv()

        @pl.loop(0, 2)
        def _(e):
            row_pos = lax.broadcasted_iota(jnp.int32, (TOK, KEYS), 0) + SPAN * TOK
            key_pos = lax.broadcasted_iota(jnp.int32, (TOK, KEYS), 1)
            allowed = (qid_ref[e] == kid_ref[e]) & (key_pos <= row_pos)
            bias[...] = jnp.where(allowed, 0.0, masked_score)
            k = lkv[e, :, 0].reshape(KEYS, HEAD)
            v = lkv[e, :, 1].reshape(KEYS, HEAD)
            va = jnp.concatenate([v, jnp.ones((KEYS, HEAD), jnp.bfloat16)], axis=1)
            for h in range(GROUP):
                cols = slice(h * HEAD, (h + 1) * HEAD)
                s = lax.dot_general(
                    lq_buf[e, :, cols], k, (((1,), (1,)), ((), ())),
                    preferred_element_type=jnp.float32,
                )
                p = jnp.exp2(s * (scaling * log2e) + bias[...]).astype(jnp.bfloat16)
                o = jnp.dot(p, va, preferred_element_type=jnp.float32)
                ol_buf[e, :, cols] = (o[:, :HEAD] / o[:, HEAD:]).astype(jnp.bfloat16)

        send(OL)

    def unit(eq, ek, zs, ys, start=None, slope=None):
        k = jnp.concatenate([kv[ek, zs[n], ys[n], 0] for n in range(4)], axis=0)
        v = jnp.concatenate([kv[ek, zs[n], ys[n], 1] for n in range(4)], axis=0)
        kk = jnp.concatenate([k, k], axis=1)
        va = jnp.concatenate([v, jnp.ones((CHUNK, HEAD), jnp.bfloat16)], axis=1)
        for t in range(ROWS // TILE):
            rows = pl.ds(t * TILE, TILE)
            s = lax.dot_general(
                qs[eq, rows, :], kk, (((1,), (1,)), ((), ())),
                preferred_element_type=jnp.float32,
            )
            if start is not None:
                r = t * TILE + lax.broadcasted_iota(jnp.int32, (TILE, HEAD), 0)
                for h in range(GROUP - 1, 0, -1):
                    r = jnp.where(r >= h * TOK, r - h * TOK, r)
                limit = tiled(r * slope + start, CHUNK // HEAD)
                key = lax.broadcasted_iota(jnp.int32, (TILE, CHUNK), 1)
                s = jnp.where(key <= limit, s, masked_score)
            before = m_ref[eq, rows, :]
            peak = jnp.maximum(before, jnp.max(s, axis=1, keepdims=True))
            factor = jnp.exp2(before - peak)
            p = jnp.exp2(s - tiled(peak, CHUNK // HEAD)).astype(jnp.bfloat16)
            acc[eq, rows, :] = acc[eq, rows, :] * tiled(factor, 2) + jnp.dot(
                p, va, preferred_element_type=jnp.float32
            )
            m_ref[eq, rows, :] = peak

    def finish(e):
        for h in range(GROUP):
            o = acc[e, h * TOK : (h + 1) * TOK, :]
            og_buf[e, :, h * HEAD : (h + 1) * HEAD] = (o[:, :HEAD] / o[:, HEAD:]).astype(
                jnp.bfloat16
            )
        send_global(e)

    def service_1():
        arrived(late_z, 3)
        begin(late_z, 4)
        begin(late_first, 5, 6)
        received(KL)
        received(VL)

        @pl.loop(1, SPAN + 1)
        def _(d):
            halo(d, 0).start()
            halo(d, 1).start()

        send(QL)
        arrived(early_first, 0, 1, 2, 3)
        begin(early_z, 2)

    def service_2():
        arrived(late_z, 4)
        begin(late_first, 7)

    def service_3():
        for i in range(5):
            arrived(late_first, i)
            begin(late_second, i)

    def service_4():
        arrived(early_z, 2)
        begin(early_z, 3)
        for i in range(5, 8):
            arrived(late_first, i)
            begin(late_second, i)

    def service_8():
        arrived(early_z, 3)
        begin(early_z, 4)

    def service_10():
        local_attention()
        arrived(early_z, 4)

    def service_11():
        finish(0)
        arrived(late_second, *range(8))

    services = {
        1: service_1,
        2: service_2,
        3: service_3,
        4: service_4,
        8: service_8,
        10: service_10,
        11: service_11,
    }

    @pl.loop(0, 24)
    def _(j):
        pair = j // 2
        second = lax.rem(j, 2)
        for at_pair, action in services.items():
            pl.when(j == 2 * at_pair)(action)

        column = (pair == 3) | (pair == 6) | (pair == 7) | (pair == 11)
        i = jnp.where(pair < 3, pair, jnp.where(pair < 6, pair - 1, pair - 3))
        away = (i + 1) // 2
        chunk = lax.rem(z + jnp.where(lax.rem(i, 2) == 1, 8 - away, away), NZ)
        turn = jnp.where(pair == 3, 0, jnp.where(pair == 6, 3, jnp.where(pair == 7, 1, 2)))
        y_col = lax.rem(y + turn, NY)
        z_rel = z - 4 * second

        early_query = jnp.logical_not(column) & (second == 1)
        eq = jnp.where(early_query, 0, 1)
        ek = jnp.where(column, 1, 0)
        do = jnp.where(column, z_rel >= 0, (second == 0) | (chunk <= z))
        masked = jnp.where(column, z_rel <= 3, (second == 1) & (chunk == z))
        slope = jnp.where(column & (y_col != y), 0, 1)
        start = jnp.where(
            column,
            z_rel * TOK + jnp.where(y_col < y, TOK - 1, jnp.where(y_col == y, 0, -1)),
            y * TOK,
        )
        zs = [jnp.where(column, 4 * second + n, chunk) for n in range(4)]
        ys = [jnp.where(column, y_col, n) for n in range(4)]

        @pl.when(do & jnp.logical_not(masked))
        def _():
            unit(eq, ek, zs, ys)

        @pl.when(do & masked)
        def _():
            unit(eq, ek, zs, ys, start, slope)

    finish(1)
    for kind in (KG, VG, KL, VL, QL, QG, OL):
        sent(kind)
    left(early_y, 1, 2)
    left(early_first, 0, 1, 2, 3)
    left(early_z, 2, 3, 4)
    left(late_z, 1, 2, 3, 4)
    left(late_first, *range(8))
    left(late_second, *range(8))

    @pl.loop(1, SPAN + 1)
    def _(d):
        halo(d, 0).wait_send()
        halo(d, 1).wait_send()

    received(OL)
    received(OG)
    sent(OG)


def shards(
    query_local, key_local, value_local, stretch_labels, query_global, key_global, value_global
):
    ctx = lax.axis_index("ctx")
    head = lax.axis_index("head")
    c = ctx % 32
    positions = (ctx * TOK + head * OWN + jnp.arange(OWN, dtype=jnp.int32)).astype(jnp.float32)
    half = HEAD // 2
    frequency = rope_base ** (-(jnp.arange(half, dtype=jnp.float32) * 2.0 / HEAD))
    angles = positions[:, None] * frequency[None, :]
    cosine, sine = jnp.cos(angles), jnp.sin(angles)
    cosine = jnp.concatenate([cosine, cosine], axis=1)
    sine = jnp.concatenate([-sine, sine], axis=1)
    padded = jnp.concatenate([jnp.full((SPAN * TOK,), -1, jnp.int32), stretch_labels])
    kid = jnp.stack(
        [lax.dynamic_slice_in_dim(padded, (32 * e + c) * TOK, KEYS, 0) for e in range(2)]
    )
    qid = kid[:, SPAN * TOK :].reshape(2, TOK, 1)
    kid = kid.reshape(2, 1, KEYS)
    any_space = pl.BlockSpec(memory_space=pl.ANY)
    vmem = pl.BlockSpec(memory_space=pltpu.VMEM)
    bf16, f32 = jnp.bfloat16, jnp.float32
    out = jax.ShapeDtypeStruct(query_local.shape, bf16)
    return pl.pallas_call(
        kernel,
        out_shape=(out, out),
        in_specs=[any_space] * 6 + [vmem] * 4,
        out_specs=(any_space, any_space),
        scratch_shapes=[
            pltpu.VMEM((OWN, 8 * WIDE), bf16),
            pltpu.VMEM((OWN, 8 * HEAD), bf16),
            pltpu.VMEM((2, NZ, NY, 2, TOK, HEAD), bf16),
            pltpu.VMEM((2, SPAN + 1, 2, TOK, HEAD), bf16),
            pltpu.VMEM((2, TOK, WIDE), bf16),
            pltpu.VMEM((2, TOK, WIDE), bf16),
            pltpu.VMEM((OWN, 8 * WIDE), bf16),
            pltpu.VMEM((OWN, 8 * HEAD), bf16),
            pltpu.VMEM((2, ROWS, 2 * HEAD), bf16),
            pltpu.VMEM((2, ROWS, HEAD), f32),
            pltpu.VMEM((2, ROWS, 2 * HEAD), f32),
            pltpu.VMEM((2, TOK, WIDE), bf16),
            pltpu.VMEM((2, TOK, WIDE), bf16),
            pltpu.VMEM((TOK, KEYS), f32),
            pltpu.SemaphoreType.DMA((8, 8)),
            pltpu.SemaphoreType.DMA((8, 8)),
            pltpu.SemaphoreType.DMA((58,)),
            pltpu.SemaphoreType.DMA((58,)),
            pltpu.SemaphoreType.DMA((SPAN, 2)),
            pltpu.SemaphoreType.DMA((SPAN, 2)),
            pltpu.SemaphoreType.DMA((2,)),
        ],
        compiler_params=pltpu.CompilerParams(
            collective_id=0, has_side_effects=True, vmem_limit_bytes=62 << 20
        ),
    )(
        query_local, key_local, value_local, query_global, key_global, value_global,
        cosine, sine, kid, qid,
    )


def solution(mesh):
    rows = P(("ctx", "head"), None)
    return jax.shard_map(
        shards,
        mesh=mesh,
        in_specs=(rows, rows, rows, P(), rows, rows, rows),
        out_specs=(rows, rows),
        check_vma=False,
    )
```

time: 143 us -> 95 us (0.66)
  the two profiles are of different devices: /device:TPU:1 before, /device:TPU:217 now
where the time goes in v2:
time: 95 us; the launch traced here: 94.8 us
  Pallas kernels  88.3 us (93%)
  local copies, waits for them, and re-layouts  4.94 us (5%)
    pallas_call x1, Pallas kernels, shards(): pl.pallas_call(kernel, out_shape=(out, out), in_specs=[any_space] * 6 + [...  88.3 us
    unnamed x6, local copies, waits for them, and re-layouts  3.42 us

profile of v2, /device:TPU:217, one launch (start us, length us, event | category | flops | bytes accessed | tf_op | source)
XLA Modules:
  0.0 94.8 jit_solution(1633854587393721956)
XLA Ops:
  0.6 0.0 copy-start.1
  0.7 0.7 copy-done.1
  1.4 0.1 pad_dynamic-slice_fusion.1
  1.5 0.6 reshape.21.kid_ref
  2.2 0.2 fusion
  2.3 0.7 pad_maximum_fusion
  3.0 0.8 copy.10.qid_ref
  3.9 88.3 %shard_map.86 = (bf16[48,5120]{1,0:T(8,128)(2,1)}, bf16[48,5120]{1,0:T(8,128)(2,1)}) custom-call(bf16[48,5120]{1,0:T(8,128)(2,1)} %ql_hbm.1, bf16[48,1024]{1,0:T(8,128)(2,1)} %kl_hbm.1, bf16[48,1024]{1,0:T(8,128)(2,1)} %vl_hbm.1, bf16[48,5120]{1,0:T(8,128)(2,1)} %qg_hbm.1, bf16[48,1024]{1,0:T(8,128)(2,1)} %kg_hbm.1, bf16[48,1024]{1,0:T(8,128)(2,1)} %vg_hbm.1, ...), custom_call_target="tpu_custom_call" | custom-call | tf_op jit(solution)/shard_map/pallas_call | solution.py:485
  92.1 0.0 copy-start
  92.1 1.9 %copy.13 = bf16[48,5120]{1,0:T(8,128)(2,1)} copy(bf16[48,5120]{1,0:T(8,128)(2,1)} %get-tuple-element.11) | data formatting | bytes 983040
  94.0 0.0 copy-done
  94.0 0.8 copy.14
  (4 shorter events, 0.0 us)
Async XLA Ops:
  0.6 0.8 copy-start.1
  92.1 1.9 %copy-start = (bf16[48,5120]{1,0:T(8,128)(2,1)S(1)}, bf16[48,5120]{1,0:T(8,128)(2,1)}, u32[]{:S(2)}) copy-start(bf16[48,5120]{1,0:T(8,128)(2,1)} %get-tuple-element.12) | copy-start | bytes 1474564

commit v3 on v2

--- a/solution.py
+++ b/solution.py
@@ -36,9 +36,9 @@
 
 
 def kernel(
-    ql_hbm, kl_hbm, vl_hbm, qg_hbm, kg_hbm, vg_hbm, cos_ref, sin_ref, kid_ref, qid_ref,
+    ql_hbm, kl_hbm, vl_hbm, qg_hbm, kg_hbm, vg_hbm, cos_ref, sin_ref, label_hbm,
     ol_hbm, og_hbm,
-    ql_ref, kl_ref, kv, lkv, qg_buf, lq_buf, nq, nk, qs, m_ref, acc, og_buf, ol_buf, bias,
+    ql_ref, kl_ref, labels, kv, lkv, qg_buf, lq_buf, nq, nk, qs, m_ref, acc, og_buf, ol_buf, bias,
     a2a_send, a2a_recv, ring_send, ring_recv, halo_send, halo_recv, load_sem,
 ):
     ctx = lax.axis_index("ctx")
@@ -71,16 +71,15 @@
         greet(line(z * NY + wrap(y + s, NY)))
         greet(line(wrap(z + s, NZ) * NY + y))
 
-    @pl.loop(1, SPAN + 1)
-    def _(t):
-        greet(line(lax.rem(c + t, 32)))
-        greet(line(lax.rem(c - t + 32, 32)))
-
     load_k = pltpu.make_async_copy(kl_hbm, kl_ref, load_sem.at[0])
     load_q = pltpu.make_async_copy(ql_hbm, ql_ref, load_sem.at[1])
+    labels[:8, :] = jnp.full((8, HEAD), -1, jnp.int32)
+    labels[104:, :] = jnp.full((8, HEAD), -1, jnp.int32)
+    load_l = pltpu.make_async_copy(label_hbm, labels.at[8:104, :], load_sem.at[2])
+    load_l.start()
     load_k.start()
     load_q.start()
-    pl.semaphore_wait(barrier, 19)
+    pl.semaphore_wait(barrier, 11)
 
     my_rows = pl.ds(head * OWN, OWN)
 
@@ -184,6 +183,8 @@
 
     def early_z(step, s):
         ref = kv.at[0, wrap(z - s * (step - 1), NZ)]
+        if step == 4:
+            ref = kv.at[0, wrap(z - s * (step - 1), NZ), :, 0 if s == 1 else 1]
         return hop(4 + 2 * (step - 2) + (s == 1), ref, z_next(s))
 
     def late_z(step, s):
@@ -198,7 +199,7 @@
         return hop(42 + 2 * i + (s == 1), ref, y_next(s))
 
     def ways(family, step):
-        return (-1,) if family in (early_z, late_z) and step == 4 else (1, -1)
+        return (-1,) if family in (late_z,) and step == 4 else (1, -1)
 
     def begin(family, *steps):
         for step in steps:
@@ -215,17 +216,57 @@
             for s in ways(family, step):
                 family(step, s).wait_send()
 
-    def halo(d, e):
-        row = lax.rem(c + d, 32)
-        other = jnp.where(c + d >= 32, 1 - e, e)
+    def halo_plane(e):
         return pltpu.make_async_remote_copy(
             src_ref=lkv.at[e, SPAN],
-            dst_ref=lkv.at[other, SPAN - d],
-            send_sem=halo_send.at[d - 1, e],
-            recv_sem=halo_recv.at[d - 1, other],
-            device_id=line(row),
+            dst_ref=lkv.at[jnp.where(z == NZ - 1, 1 - e, e), 0],
+            send_sem=halo_send.at[e],
+            recv_sem=halo_recv.at[jnp.where(z == NZ - 1, 1 - e, e)],
+            device_id=z_next(1),
             device_id_type=MESH,
         )
+
+    def halo_side(number, landing, source, target, s):
+        return pltpu.make_async_remote_copy(
+            src_ref=lkv.at[:, source],
+            dst_ref=lkv.at[:, target],
+            send_sem=halo_send.at[number],
+            recv_sem=halo_recv.at[landing],
+            device_id=y_next(s),
+            device_id_type=MESH,
+        )
+
+    def halo_up():
+        return halo_side(2, 2, jnp.where(y == NY - 1, 0, SPAN), SPAN - 1, 1)
+
+    def halo_down():
+        return halo_side(3, 3, jnp.where(y == 0, SPAN, 0), SPAN - 3, -1)
+
+    def halo_on(s):
+        return halo_side(4 + (s == 1), 4, SPAN - 1 if s == 1 else SPAN - 3, SPAN - 2, s)
+
+    inner = (y == 1) | (y == 2)
+
+    def halo_1():
+        for e in range(2):
+            halo_plane(e).start()
+        pl.when(y != NY - 1)(lambda: halo_up().start())
+        pl.when(y == 0)(lambda: halo_down().start())
+
+    def halo_2():
+        for e in range(2):
+            halo_plane(e).wait_recv()
+        pl.when(y == NY - 1)(lambda: halo_up().start())
+        pl.when(y != 0)(lambda: halo_down().start())
+
+    def halo_3():
+        halo_up().wait_recv()
+        halo_down().wait_recv()
+
+        @pl.when(inner)
+        def _():
+            halo_on(1).start()
+            halo_on(-1).start()
 
     def normalized(x):
         x = x.astype(jnp.float32)
@@ -249,6 +290,25 @@
 
     m_ref[...] = jnp.full(m_ref.shape, masked_score, jnp.float32)
     acc[...] = jnp.zeros(acc.shape, jnp.float32)
+    load_l.wait()
+
+    @pl.loop(0, 2)
+    def _(e):
+        first = 8 * HEAD + (32 * e + c - SPAN) * TOK
+        wide = jnp.concatenate(
+            [labels[pl.ds(first // HEAD + n, 1), :] for n in range(9)], axis=1
+        ).astype(jnp.float32)
+        shifted = pltpu.roll(wide, 9 * HEAD - HEAD // 2, 1)
+        wide = jnp.where(lax.rem(c, 2) == 1, shifted, wide)
+        own = wide[:, SPAN * TOK : 8 * HEAD]
+        row = lax.broadcasted_iota(jnp.int32, (TOK, 2 * HEAD), 0)
+        col = lax.broadcasted_iota(jnp.int32, (TOK, 2 * HEAD), 1)
+        mine = jnp.sum(jnp.where(row == col, own, 0.0), axis=1, keepdims=True)
+        row_pos = lax.broadcasted_iota(jnp.int32, (TOK, KEYS), 0) + SPAN * TOK
+        key_pos = lax.broadcasted_iota(jnp.int32, (TOK, KEYS), 1)
+        allowed = (wide[:, :KEYS] == mine) & (key_pos <= row_pos)
+        bias[e] = jnp.where(allowed, 0.0, masked_score)
+
     received(KG)
     received(VG)
     begin(late_z, 1)
@@ -286,18 +346,10 @@
 
     def local_attention():
         received(QL)
-
-        @pl.loop(1, SPAN + 1)
-        def _(d):
-            halo(d, 0).wait_recv()
-            halo(d, 1).wait_recv()
+        halo_on(1).wait_recv()
 
         @pl.loop(0, 2)
         def _(e):
-            row_pos = lax.broadcasted_iota(jnp.int32, (TOK, KEYS), 0) + SPAN * TOK
-            key_pos = lax.broadcasted_iota(jnp.int32, (TOK, KEYS), 1)
-            allowed = (qid_ref[e] == kid_ref[e]) & (key_pos <= row_pos)
-            bias[...] = jnp.where(allowed, 0.0, masked_score)
             k = lkv[e, :, 0].reshape(KEYS, HEAD)
             v = lkv[e, :, 1].reshape(KEYS, HEAD)
             va = jnp.concatenate([v, jnp.ones((KEYS, HEAD), jnp.bfloat16)], axis=1)
@@ -307,7 +359,7 @@
                     lq_buf[e, :, cols], k, (((1,), (1,)), ((), ())),
                     preferred_element_type=jnp.float32,
                 )
-                p = jnp.exp2(s * (scaling * log2e) + bias[...]).astype(jnp.bfloat16)
+                p = jnp.exp2(s * (scaling * log2e) + bias[e]).astype(jnp.bfloat16)
                 o = jnp.dot(p, va, preferred_element_type=jnp.float32)
                 ol_buf[e, :, cols] = (o[:, :HEAD] / o[:, HEAD:]).astype(jnp.bfloat16)
 
@@ -352,21 +404,17 @@
         arrived(late_z, 3)
         begin(late_z, 4)
         begin(late_first, 5, 6)
+        arrived(early_first, 0, 1, 2, 3)
+        begin(early_z, 2)
         received(KL)
         received(VL)
-
-        @pl.loop(1, SPAN + 1)
-        def _(d):
-            halo(d, 0).start()
-            halo(d, 1).start()
-
+        halo_1()
         send(QL)
-        arrived(early_first, 0, 1, 2, 3)
-        begin(early_z, 2)
 
     def service_2():
         arrived(late_z, 4)
         begin(late_first, 7)
+        halo_2()
 
     def service_3():
         for i in range(5):
@@ -379,13 +427,14 @@
         for i in range(5, 8):
             arrived(late_first, i)
             begin(late_second, i)
+        halo_3()
 
     def service_8():
         arrived(early_z, 3)
         begin(early_z, 4)
+        local_attention()
 
     def service_10():
-        local_attention()
         arrived(early_z, 4)
 
     def service_11():
@@ -448,11 +497,15 @@
     left(late_z, 1, 2, 3, 4)
     left(late_first, *range(8))
     left(late_second, *range(8))
-
-    @pl.loop(1, SPAN + 1)
-    def _(d):
-        halo(d, 0).wait_send()
-        halo(d, 1).wait_send()
+    for e in range(2):
+        halo_plane(e).wait_send()
+    halo_up().wait_send()
+    halo_down().wait_send()
+
+    @pl.when(inner)
+    def _():
+        halo_on(1).wait_send()
+        halo_on(-1).wait_send()
 
     received(OL)
     received(OG)
@@ -464,7 +517,6 @@
 ):
     ctx = lax.axis_index("ctx")
     head = lax.axis_index("head")
-    c = ctx % 32
     positions = (ctx * TOK + head * OWN + jnp.arange(OWN, dtype=jnp.int32)).astype(jnp.float32)
     half = HEAD // 2
     frequency = rope_base ** (-(jnp.arange(half, dtype=jnp.float32) * 2.0 / HEAD))
@@ -472,12 +524,6 @@
     cosine, sine = jnp.cos(angles), jnp.sin(angles)
     cosine = jnp.concatenate([cosine, cosine], axis=1)
     sine = jnp.concatenate([-sine, sine], axis=1)
-    padded = jnp.concatenate([jnp.full((SPAN * TOK,), -1, jnp.int32), stretch_labels])
-    kid = jnp.stack(
-        [lax.dynamic_slice_in_dim(padded, (32 * e + c) * TOK, KEYS, 0) for e in range(2)]
-    )
-    qid = kid[:, SPAN * TOK :].reshape(2, TOK, 1)
-    kid = kid.reshape(2, 1, KEYS)
     any_space = pl.BlockSpec(memory_space=pl.ANY)
     vmem = pl.BlockSpec(memory_space=pltpu.VMEM)
     bf16, f32 = jnp.bfloat16, jnp.float32
@@ -485,11 +531,12 @@
     return pl.pallas_call(
         kernel,
         out_shape=(out, out),
-        in_specs=[any_space] * 6 + [vmem] * 4,
+        in_specs=[any_space] * 6 + [vmem] * 2 + [any_space],
         out_specs=(any_space, any_space),
         scratch_shapes=[
             pltpu.VMEM((OWN, 8 * WIDE), bf16),
             pltpu.VMEM((OWN, 8 * HEAD), bf16),
+            pltpu.VMEM((112, HEAD), jnp.int32),
             pltpu.VMEM((2, NZ, NY, 2, TOK, HEAD), bf16),
             pltpu.VMEM((2, SPAN + 1, 2, TOK, HEAD), bf16),
             pltpu.VMEM((2, TOK, WIDE), bf16),
@@ -501,21 +548,21 @@
             pltpu.VMEM((2, ROWS, 2 * HEAD), f32),
             pltpu.VMEM((2, TOK, WIDE), bf16),
             pltpu.VMEM((2, TOK, WIDE), bf16),
-            pltpu.VMEM((TOK, KEYS), f32),
+            pltpu.VMEM((2, TOK, KEYS), f32),
             pltpu.SemaphoreType.DMA((8, 8)),
             pltpu.SemaphoreType.DMA((8, 8)),
             pltpu.SemaphoreType.DMA((58,)),
             pltpu.SemaphoreType.DMA((58,)),
-            pltpu.SemaphoreType.DMA((SPAN, 2)),
-            pltpu.SemaphoreType.DMA((SPAN, 2)),
-            pltpu.SemaphoreType.DMA((2,)),
+            pltpu.SemaphoreType.DMA((6,)),
+            pltpu.SemaphoreType.DMA((5,)),
+            pltpu.SemaphoreType.DMA((3,)),
         ],
         compiler_params=pltpu.CompilerParams(
             collective_id=0, has_side_effects=True, vmem_limit_bytes=62 << 20
         ),
     )(
         query_local, key_local, value_local, query_global, key_global, value_global,
-        cosine, sine, kid, qid,
+        cosine, sine, stretch_labels.reshape(-1, HEAD),
     )
 
 

time: 95 us -> 86.7 us (0.913)
  the two profiles are of different devices: /device:TPU:217 before, /device:TPU:131 now
where the time goes in v3:
time: 86.7 us; the launch traced here: 85 us
  Pallas kernels  80.8 us (93%)
  local copies, waits for them, and re-layouts  2.68 us (3%)
  other arithmetic  0.89 us (1%)
    pallas_call x1, Pallas kernels, shards(): pl.pallas_call(kernel, out_shape=(out, out), in_specs=[any_space] * 6 + [...  80.8 us
    unnamed x4, local copies, waits for them, and re-layouts  2.68 us

profile of v3, /device:TPU:131, one launch (start us, length us, event | category | flops | bytes accessed | tf_op | source)
XLA Modules:
  0.0 85.0 jit_solution(1857299595285852753)
XLA Ops:
  0.7 0.2 fusion
  0.8 0.7 pad_maximum_fusion
  1.5 80.8 %shard_map.86 = (bf16[48,5120]{1,0:T(8,128)(2,1)}, bf16[48,5120]{1,0:T(8,128)(2,1)}) custom-call(bf16[48,5120]{1,0:T(8,128)(2,1)} %ql_hbm.1, bf16[48,1024]{1,0:T(8,128)(2,1)} %kl_hbm.1, bf16[48,1024]{1,0:T(8,128)(2,1)} %vl_hbm.1, bf16[48,5120]{1,0:T(8,128)(2,1)} %qg_hbm.1, bf16[48,1024]{1,0:T(8,128)(2,1)} %kg_hbm.1, bf16[48,1024]{1,0:T(8,128)(2,1)} %vg_hbm.1, ...), custom_call_target="tpu_custom_call" | custom-call | tf_op jit(solution)/shard_map/pallas_call | solution.py:531
  82.4 0.0 copy-start
  82.4 1.9 %copy.11 = bf16[48,5120]{1,0:T(8,128)(2,1)} copy(bf16[48,5120]{1,0:T(8,128)(2,1)} %get-tuple-element.9) | data formatting | bytes 983040
  84.3 0.0 copy-done
  84.3 0.8 copy.12
  (2 shorter events, 0.0 us)
Async XLA Ops:
  82.4 1.9 %copy-start = (bf16[48,5120]{1,0:T(8,128)(2,1)S(1)}, bf16[48,5120]{1,0:T(8,128)(2,1)}, u32[]{:S(2)}) copy-start(bf16[48,5120]{1,0:T(8,128)(2,1)} %get-tuple-element.10) | copy-start | bytes 1474564

commit v4 on v3

--- a/solution.py
+++ b/solution.py
@@ -366,27 +366,36 @@
         send(OL)
 
     def unit(eq, ek, zs, ys, start=None, slope=None):
-        k = jnp.concatenate([kv[ek, zs[n], ys[n], 0] for n in range(4)], axis=0)
-        v = jnp.concatenate([kv[ek, zs[n], ys[n], 1] for n in range(4)], axis=0)
+        keys = TOK * len(zs)
+        k = jnp.concatenate([kv[ek, a, b, 0] for a, b in zip(zs, ys)], axis=0)
+        v = jnp.concatenate([kv[ek, a, b, 1] for a, b in zip(zs, ys)], axis=0)
         kk = jnp.concatenate([k, k], axis=1)
-        va = jnp.concatenate([v, jnp.ones((CHUNK, HEAD), jnp.bfloat16)], axis=1)
+        va = jnp.concatenate([v, jnp.ones((keys, HEAD), jnp.bfloat16)], axis=1)
+
+        def scores(t):
+            return lax.dot_general(
+                qs[eq, t * TILE : (t + 1) * TILE, :], kk, (((1,), (1,)), ((), ())),
+                preferred_element_type=jnp.float32,
+            )
+
+        ahead = scores(0)
         for t in range(ROWS // TILE):
             rows = pl.ds(t * TILE, TILE)
-            s = lax.dot_general(
-                qs[eq, rows, :], kk, (((1,), (1,)), ((), ())),
-                preferred_element_type=jnp.float32,
-            )
+            s = ahead
+            if t + 1 < ROWS // TILE:
+                ahead = scores(t + 1)
             if start is not None:
                 r = t * TILE + lax.broadcasted_iota(jnp.int32, (TILE, HEAD), 0)
                 for h in range(GROUP - 1, 0, -1):
                     r = jnp.where(r >= h * TOK, r - h * TOK, r)
-                limit = tiled(r * slope + start, CHUNK // HEAD)
+                limit = tiled(r * slope + (start - (keys - CHUNK)), CHUNK // HEAD)
                 key = lax.broadcasted_iota(jnp.int32, (TILE, CHUNK), 1)
-                s = jnp.where(key <= limit, s, masked_score)
+                last = jnp.where(key <= limit, s[:, keys - CHUNK :], masked_score)
+                s = last if keys == CHUNK else jnp.concatenate([s[:, : keys - CHUNK], last], 1)
             before = m_ref[eq, rows, :]
             peak = jnp.maximum(before, jnp.max(s, axis=1, keepdims=True))
             factor = jnp.exp2(before - peak)
-            p = jnp.exp2(s - tiled(peak, CHUNK // HEAD)).astype(jnp.bfloat16)
+            p = jnp.exp2(s - tiled(peak, keys // HEAD)).astype(jnp.bfloat16)
             acc[eq, rows, :] = acc[eq, rows, :] * tiled(factor, 2) + jnp.dot(
                 p, va, preferred_element_type=jnp.float32
             )
@@ -442,49 +451,59 @@
         arrived(late_second, *range(8))
 
     services = {
-        1: service_1,
-        2: service_2,
-        3: service_3,
-        4: service_4,
-        8: service_8,
-        10: service_10,
-        11: service_11,
+        2: service_1,
+        3: service_2,
+        4: service_3,
+        6: service_4,
+        12: service_8,
+        14: service_10,
+        16: service_11,
     }
 
-    @pl.loop(0, 24)
+    @pl.loop(0, 17)
     def _(j):
-        pair = j // 2
-        second = lax.rem(j, 2)
-        for at_pair, action in services.items():
-            pl.when(j == 2 * at_pair)(action)
-
-        column = (pair == 3) | (pair == 6) | (pair == 7) | (pair == 11)
-        i = jnp.where(pair < 3, pair, jnp.where(pair < 6, pair - 1, pair - 3))
-        away = (i + 1) // 2
-        chunk = lax.rem(z + jnp.where(lax.rem(i, 2) == 1, 8 - away, away), NZ)
-        turn = jnp.where(pair == 3, 0, jnp.where(pair == 6, 3, jnp.where(pair == 7, 1, 2)))
+        slot = j // 2
+        second = lax.rem(j, 2) == 1
+        for place, action in services.items():
+            pl.when(j == place)(action)
+
+        column = (slot == 2) | (slot == 4) | (slot == 5) | (slot == 8)
+        far = jnp.where(slot < 2, slot, jnp.where(slot == 3, 2, slot - 3))
+        below = lax.rem(z - far + NZ, NZ)
+        above = lax.rem(z + far, NZ)
+        turn = jnp.where(slot == 2, 0, jnp.where(slot == 4, 3, jnp.where(slot == 5, 1, 2)))
         y_col = lax.rem(y + turn, NY)
-        z_rel = z - 4 * second
-
-        early_query = jnp.logical_not(column) & (second == 1)
-        eq = jnp.where(early_query, 0, 1)
+
+        two = (far > 0) & (far < 4)
+        wide = jnp.where(column, z >= 4, two & (jnp.logical_not(second) | (z + far >= NZ)))
+        do = jnp.where(column, jnp.logical_not(second), jnp.logical_not(second) | (z >= far))
+        masked = column | (second & (far == 0))
+        eq = jnp.where(jnp.logical_not(column) & second, 0, 1)
         ek = jnp.where(column, 1, 0)
-        do = jnp.where(column, z_rel >= 0, (second == 0) | (chunk <= z))
-        masked = jnp.where(column, z_rel <= 3, (second == 1) & (chunk == z))
         slope = jnp.where(column & (y_col != y), 0, 1)
         start = jnp.where(
             column,
-            z_rel * TOK + jnp.where(y_col < y, TOK - 1, jnp.where(y_col == y, 0, -1)),
+            z * TOK + jnp.where(y_col < y, TOK - 1, jnp.where(y_col == y, 0, -1)),
             y * TOK,
         )
-        zs = [jnp.where(column, 4 * second + n, chunk) for n in range(4)]
-        ys = [jnp.where(column, y_col, n) for n in range(4)]
-
-        @pl.when(do & jnp.logical_not(masked))
+        zs = [jnp.where(column, n, below if n < 4 else above) for n in range(8)]
+        ys = [jnp.where(column, y_col, n % 4) for n in range(8)]
+        free = jnp.logical_not(masked)
+        narrow = jnp.logical_not(wide)
+
+        @pl.when(do & narrow & free)
+        def _():
+            unit(eq, ek, zs[:4], ys[:4])
+
+        @pl.when(do & narrow & masked)
+        def _():
+            unit(eq, ek, zs[:4], ys[:4], start, slope)
+
+        @pl.when(do & wide & free)
         def _():
             unit(eq, ek, zs, ys)
 
-        @pl.when(do & masked)
+        @pl.when(do & wide & masked)
         def _():
             unit(eq, ek, zs, ys, start, slope)
 

time: 86.7 us -> 81.2 us (0.937); the launches traced: 85 us -> 81.1 us
  Pallas kernels: 80.8 us -> 76.8 us
    pallas_call x1, Pallas kernels: 80.8 us -> 76.8 us  [shards(): pl.pallas_call(kernel, out_shape=(out, out), in_specs=[any_space] * 6 + [...]
where the time goes in v4:
time: 81.2 us; the launch traced here: 81.1 us
  Pallas kernels  76.8 us (95%)
  local copies, waits for them, and re-layouts  2.68 us (3%)
  other arithmetic  0.89 us (1%)
    pallas_call x1, Pallas kernels, shards(): pl.pallas_call(kernel, out_shape=(out, out), in_specs=[any_space] * 6 + [...  76.8 us
    unnamed x4, local copies, waits for them, and re-layouts  2.68 us

profile of v4, /device:TPU:131, one launch (start us, length us, event | category | flops | bytes accessed | tf_op | source)
XLA Modules:
  0.0 81.1 jit_solution(14774060819314203308)
XLA Ops:
  0.7 0.2 fusion
  0.8 0.7 pad_maximum_fusion
  1.5 76.8 %shard_map.86 = (bf16[48,5120]{1,0:T(8,128)(2,1)}, bf16[48,5120]{1,0:T(8,128)(2,1)}) custom-call(bf16[48,5120]{1,0:T(8,128)(2,1)} %ql_hbm.1, bf16[48,1024]{1,0:T(8,128)(2,1)} %kl_hbm.1, bf16[48,1024]{1,0:T(8,128)(2,1)} %vl_hbm.1, bf16[48,5120]{1,0:T(8,128)(2,1)} %qg_hbm.1, bf16[48,1024]{1,0:T(8,128)(2,1)} %kg_hbm.1, bf16[48,1024]{1,0:T(8,128)(2,1)} %vg_hbm.1, ...), custom_call_target="tpu_custom_call" | custom-call | tf_op jit(solution)/shard_map/pallas_call | solution.py:550
  78.4 0.0 copy-start
  78.4 1.9 %copy.11 = bf16[48,5120]{1,0:T(8,128)(2,1)} copy(bf16[48,5120]{1,0:T(8,128)(2,1)} %get-tuple-element.9) | data formatting | bytes 983040
  80.3 0.0 copy-done
  80.3 0.8 copy.12
  (2 shorter events, 0.0 us)
Async XLA Ops:
  78.4 1.9 %copy-start = (bf16[48,5120]{1,0:T(8,128)(2,1)S(1)}, bf16[48,5120]{1,0:T(8,128)(2,1)}, u32[]{:S(2)}) copy-start(bf16[48,5120]{1,0:T(8,128)(2,1)} %get-tuple-element.10) | copy-start | bytes 1474564

commit v5 on v4

--- a/solution.py
+++ b/solution.py
@@ -36,9 +36,9 @@
 
 
 def kernel(
-    ql_hbm, kl_hbm, vl_hbm, qg_hbm, kg_hbm, vg_hbm, cos_ref, sin_ref, label_hbm,
+    ql_hbm, kl_hbm, vl_hbm, qg_hbm, kg_hbm, vg_hbm, cos_hbm, sin_hbm, label_hbm,
     ol_hbm, og_hbm,
-    ql_ref, kl_ref, labels, kv, lkv, qg_buf, lq_buf, nq, nk, qs, m_ref, acc, og_buf, ol_buf, bias,
+    ql_ref, kl_ref, cos_half, sin_half, cos_ref, sin_ref, labels, kv, lkv, qg_buf, lq_buf, nq, nk, qs, m_ref, acc, og_buf, ol_buf, bias,
     a2a_send, a2a_recv, ring_send, ring_recv, halo_send, halo_recv, load_sem,
 ):
     ctx = lax.axis_index("ctx")
@@ -77,6 +77,10 @@
     labels[104:, :] = jnp.full((8, HEAD), -1, jnp.int32)
     load_l = pltpu.make_async_copy(label_hbm, labels.at[8:104, :], load_sem.at[2])
     load_l.start()
+    load_c = pltpu.make_async_copy(cos_hbm, cos_half, load_sem.at[3])
+    load_s = pltpu.make_async_copy(sin_hbm, sin_half, load_sem.at[4])
+    load_c.start()
+    load_s.start()
     load_k.start()
     load_q.start()
     pl.semaphore_wait(barrier, 11)
@@ -276,6 +280,10 @@
 
     send(KG)
     send(VG)
+    load_c.wait()
+    load_s.wait()
+    cos_ref[...] = tiled(cos_half[...], 2)
+    sin_ref[...] = jnp.concatenate([-sin_half[...], sin_half[...]], axis=1)
     load_k.wait()
     for h in range(8):
         cols = slice(h * HEAD, (h + 1) * HEAD)
@@ -288,6 +296,13 @@
             cols = pl.ds(pl.multiple_of(t * WIDE + h * HEAD, HEAD), HEAD)
             nq[:, cols] = normalized(ql_ref[:, cols])
 
+    received(KG)
+    received(VG)
+    begin(late_z, 1)
+    begin(early_y, 1)
+    begin(early_first, 0)
+    begin(late_first, 0)
+    send(QG)
     m_ref[...] = jnp.full(m_ref.shape, masked_score, jnp.float32)
     acc[...] = jnp.zeros(acc.shape, jnp.float32)
     load_l.wait()
@@ -309,13 +324,6 @@
         allowed = (wide[:, :KEYS] == mine) & (key_pos <= row_pos)
         bias[e] = jnp.where(allowed, 0.0, masked_score)
 
-    received(KG)
-    received(VG)
-    begin(late_z, 1)
-    begin(early_y, 1)
-    begin(early_first, 0)
-    begin(late_first, 0)
-    send(QG)
     arrived(early_y, 1)
     begin(early_y, 2)
     begin(early_first, 1, 2)
@@ -541,20 +549,21 @@
     frequency = rope_base ** (-(jnp.arange(half, dtype=jnp.float32) * 2.0 / HEAD))
     angles = positions[:, None] * frequency[None, :]
     cosine, sine = jnp.cos(angles), jnp.sin(angles)
-    cosine = jnp.concatenate([cosine, cosine], axis=1)
-    sine = jnp.concatenate([-sine, sine], axis=1)
     any_space = pl.BlockSpec(memory_space=pl.ANY)
-    vmem = pl.BlockSpec(memory_space=pltpu.VMEM)
     bf16, f32 = jnp.bfloat16, jnp.float32
     out = jax.ShapeDtypeStruct(query_local.shape, bf16)
     return pl.pallas_call(
         kernel,
         out_shape=(out, out),
-        in_specs=[any_space] * 6 + [vmem] * 2 + [any_space],
+        in_specs=[any_space] * 9,
         out_specs=(any_space, any_space),
         scratch_shapes=[
             pltpu.VMEM((OWN, 8 * WIDE), bf16),
             pltpu.VMEM((OWN, 8 * HEAD), bf16),
+            pltpu.VMEM((OWN, HEAD // 2), f32),
+            pltpu.VMEM((OWN, HEAD // 2), f32),
+            pltpu.VMEM((OWN, HEAD), f32),
+            pltpu.VMEM((OWN, HEAD), f32),
             pltpu.VMEM((112, HEAD), jnp.int32),
             pltpu.VMEM((2, NZ, NY, 2, TOK, HEAD), bf16),
             pltpu.VMEM((2, SPAN + 1, 2, TOK, HEAD), bf16),
@@ -574,7 +583,7 @@
             pltpu.SemaphoreType.DMA((58,)),
             pltpu.SemaphoreType.DMA((6,)),
             pltpu.SemaphoreType.DMA((5,)),
-            pltpu.SemaphoreType.DMA((3,)),
+            pltpu.SemaphoreType.DMA((5,)),
         ],
         compiler_params=pltpu.CompilerParams(
             collective_id=0, has_side_effects=True, vmem_limit_bytes=62 << 20

time: 81.2 us -> 80.3 us (0.989)
  no operation moved by 1% of the time
where the time goes in v5:
time: 80.3 us; the launch traced here: 80.2 us
  Pallas kernels  76.1 us (95%)
  local copies, waits for them, and re-layouts  2.68 us (3%)
  other arithmetic  0.81 us (1%)
    pallas_call x1, Pallas kernels, shards(): pl.pallas_call(kernel, out_shape=(out, out), in_specs=[any_space] * 9, ou...  76.1 us
    unnamed x4, local copies, waits for them, and re-layouts  2.68 us

profile of v5, /device:TPU:131, one launch (start us, length us, event | category | flops | bytes accessed | tf_op | source)
XLA Modules:
  0.0 80.2 jit_solution(4627459463896621438)
XLA Ops:
  0.7 0.8 multiply_sine_fusion
  1.5 76.1 %shard_map.86 = (bf16[48,5120]{1,0:T(8,128)(2,1)}, bf16[48,5120]{1,0:T(8,128)(2,1)}) custom-call(bf16[48,5120]{1,0:T(8,128)(2,1)} %ql_hbm.1, bf16[48,1024]{1,0:T(8,128)(2,1)} %kl_hbm.1, bf16[48,1024]{1,0:T(8,128)(2,1)} %vl_hbm.1, bf16[48,5120]{1,0:T(8,128)(2,1)} %qg_hbm.1, bf16[48,1024]{1,0:T(8,128)(2,1)} %kg_hbm.1, bf16[48,1024]{1,0:T(8,128)(2,1)} %vg_hbm.1, ...), custom_call_target="tpu_custom_call" | custom-call | tf_op jit(solution)/shard_map/pallas_call | solution.py:555
  77.6 0.0 copy-start
  77.6 1.9 %copy.11 = bf16[48,5120]{1,0:T(8,128)(2,1)} copy(bf16[48,5120]{1,0:T(8,128)(2,1)} %get-tuple-element.6) | data formatting | bytes 983040
  79.5 0.0 copy-done
  79.5 0.8 copy.12
  (2 shorter events, 0.0 us)
Async XLA Ops:
  77.6 1.9 %copy-start = (bf16[48,5120]{1,0:T(8,128)(2,1)S(1)}, bf16[48,5120]{1,0:T(8,128)(2,1)}, u32[]{:S(2)}) copy-start(bf16[48,5120]{1,0:T(8,128)(2,1)} %get-tuple-element.7) | copy-start | bytes 1474564
